TPU v7x, 128 devices: a whole 4x4x4 slice. The times are simulated.
128 devices in a mesh: genome: 64 (over z, y, x), sample: 2 (over core).
Axes of the slice: x: 4, y: 4, z: 4, core: 2. Of those that a mesh axis runs over, the one named last changes fastest.
Arguments:
- genotypes: bfloat16 [32768, 8192], P('genome', 'sample'), may hold values from 0.049804688 to 2
- phenotypes: bfloat16 [4096, 8192], P('genome', 'sample'), may hold values from -60 to 60
- environment: float32 [8192], P('sample'), may hold values from 0.3 to 3
- shuffles: int32 [4, 8192], P(None, 'sample'), may hold values from 0 to 8191, each once within a row
- window_start: int32 [4096], replicated, may hold values from 0 to 127, as said below
- window_end: int32 [4096], replicated, may hold values from 1 to 128, as said below
- chrom_bounds: int32 [21], replicated, may hold values from 1 to 127, as said below
Outputs:
- maxima: float32 [5, 4096], P(None, 'genome')
Inputs may be any that keep to these rules, and one draw needn't show every extreme that they name: `window_start`: for gene g on genome index d = g // 64 the window is [c - l, c + r + 1) cut to [0, 128), where d * 2 <= c < (d + 1) * 2 and 1 <= l, r <= 7; the first gene of every index has c = d * 2 and l = 7, the last has c = (d + 1) * 2 - 1 and r = 7. `window_end`: the end of the window described for window_start. `chrom_bounds`: strictly increasing.
All inputs are finite; a program needn't handle non-finite values.
Results may differ from a plain program's by a relative error of at most 0.0024.
Values may be sent and summed in bfloat16 or wider, within the bound.
A program may use at most 128 MiB of HBM per device.

v0:
```python
import jax
import jax.numpy as jnp
from jax import lax
from jax.sharding import PartitionSpec as P

SNP_BLOCK = 256
HALF_BLK = 7


def passed_along(x, axis, by):
    count = lax.axis_size(axis)
    pairs = [(i, i + by) for i in range(count) if 0 <= i + by < count]
    return lax.ppermute(x, axis, pairs)


def window_bounds(window_start, window_end, chrom_bounds, total_blocks):
    middle = (window_start + window_end - 1) // 2
    before = chrom_bounds[None, :] <= middle[:, None]
    lower_edge = jnp.max(jnp.where(before, chrom_bounds[None, :], 0), axis=1)
    upper_edge = jnp.min(jnp.where(before, total_blocks, chrom_bounds[None, :]), axis=1)
    return (jnp.maximum(window_start, lower_edge), jnp.minimum(window_end, upper_edge))


def window_scores(reduced, square_sum, cross_sum, inter_sum):
    half_cols = reduced.shape[1] // 2
    marginal = reduced[:, :half_cols]
    interact = reduced[:, half_cols:]
    regression = cross_sum / square_sum
    resid_norm = inter_sum - cross_sum * regression
    divisor = resid_norm + 0.1 * inter_sum
    numerator = interact - regression[:, None] * marginal
    return numerator * numerator / divisor[:, None]


def label_rows(local_rows, whole_rows, shuffles):
    labels = shuffles.shape[0] + 1
    shuffled = jnp.take(whole_rows, shuffles, axis=1)
    block = jnp.concatenate([local_rows[None], jnp.transpose(shuffled, (1, 0, 2))], axis=0)
    return block.reshape(labels * local_rows.shape[0], local_rows.shape[1])


def shards(genotypes, phenotypes, environment, shuffles, window_start, window_end, chrom_bounds):
    snp_rows, local_samples = genotypes.shape
    gene_rows = phenotypes.shape[0]
    labels = shuffles.shape[0] + 1
    genome_size = lax.axis_size("genome")
    sample_size = lax.axis_size("sample")
    genome_pos = lax.axis_index("genome")
    sample_pos = lax.axis_index("sample")
    blocks_dev = snp_rows // SNP_BLOCK
    reach_dev = (HALF_BLK + blocks_dev - 1) // blocks_dev
    total_blocks = snp_rows * genome_size // SNP_BLOCK
    full_rows = lax.all_gather(phenotypes, "sample", axis=1, tiled=True)
    all_samples = full_rows.shape[1]
    row_power = jnp.sum(jnp.square(full_rows.astype(jnp.float32)), axis=1)
    own_block = label_rows(phenotypes, full_rows, shuffles)
    geno_float = genotypes.astype(jnp.float32)
    squares = geno_float * geno_float
    local_moments = jnp.stack(
        [
            jnp.sum(squares, axis=1),
            jnp.sum(squares * environment[None, :], axis=1),
            jnp.sum(squares * (environment * environment)[None, :], axis=1),
        ]
    )
    moments = lax.psum(local_moments, "sample")
    share_rows = snp_rows // sample_size
    first_row = sample_pos * share_rows
    row_moments = lax.dynamic_slice_in_dim(moments, first_row, share_rows, 1)
    row_blocks = (
        genome_pos * snp_rows + first_row + jnp.arange(share_rows, dtype=jnp.int32)
    ) // SNP_BLOCK
    lower_edge, upper_edge = window_bounds(window_start, window_end, chrom_bounds, total_blocks)
    padding = jnp.zeros((reach_dev * gene_rows,), jnp.int32)
    band_slots = 2 * reach_dev + 1
    lower_band = lax.dynamic_slice_in_dim(
        jnp.concatenate([padding, lower_edge, padding]),
        genome_pos * gene_rows,
        band_slots * gene_rows,
        0,
    ).reshape(band_slots, gene_rows)
    upper_band = lax.dynamic_slice_in_dim(
        jnp.concatenate([padding, upper_edge, padding]),
        genome_pos * gene_rows,
        band_slots * gene_rows,
        0,
    ).reshape(band_slots, gene_rows)
    pieces = {0: own_block}
    for offset in range(-reach_dev, reach_dev + 1):
        if offset != 0:
            pieces[offset] = passed_along(own_block, "genome", -offset)
    partials = []
    for offset in range(-reach_dev, reach_dev + 1):
        incoming = pieces[offset]
        weighted = (incoming.astype(jnp.float32) * environment[None, :]).astype(jnp.bfloat16)
        operand = jnp.concatenate([incoming, weighted], axis=0)

        def product(start_row, row_count, operand=operand):
            return lax.dot_general(
                genotypes, operand, (((1,), (1,)), ((), ())), preferred_element_type=jnp.float32
            )

        reduced = lax.psum_scatter(
            product(jnp.int32(0), lax.axis_size("sample") * share_rows),
            "sample",
            scatter_dimension=0,
            tiled=True,
        )
        scores = window_scores(reduced, row_moments[0], row_moments[1], row_moments[2])
        scores = scores.reshape(share_rows, labels, gene_rows)
        slot_index = offset + reach_dev
        inside = (row_blocks[:, None] >= lower_band[slot_index][None, :]) & (
            row_blocks[:, None] < upper_band[slot_index][None, :]
        )
        partials.append(jnp.max(jnp.where(inside[:, None, :], scores, 0.0), axis=0))
    stacked = lax.pmax(jnp.stack(partials), "sample")
    best_peak = stacked[reach_dev]
    for offset in range(-reach_dev, reach_dev + 1):
        if offset != 0:
            arrived = passed_along(stacked[offset + reach_dev], "genome", offset)
            best_peak = jnp.maximum(best_peak, arrived)
    return jnp.sqrt(best_peak / (row_power[None, :] / all_samples + 1e-05))


def solution(mesh):
    placed = (
        P("genome", "sample"),
        P("genome", "sample"),
        P("sample"),
        P(None, "sample"),
        P(),
        P(),
        P(),
    )
    return jax.shard_map(
        shards, mesh=mesh, in_specs=placed, out_specs=P(None, "genome"), check_vma=False
    )
```

profile of v0, /device:TPU:97, one launch (start us, length us, event | category | flops | bytes accessed | tf_op | source)
XLA Modules:
  0.0 663.1 jit_solution(12382588636542825542)
XLA Ops:
  10.8 13.4 %all-gather.2.cloned.1.call-done = bf16[64,8192]{0,1:T(8,128)(2,1)} async-done(((bf16[64,4096]{0,1:T(8,128)(2,1)}), bf16[64,8192]{0,1:T(8,128)(2,1)}) %all-gather.2.cloned.1.call-update) | async-done | bytes 1048592 | tf_op jit(solution)/shard_map/all_gather | solution.py:53
  24.2 56.8 %gather_fusion = bf16[16384,64]{1,0:T(8,128)(2,1)} fusion(bf16[64,8192]{0,1:T(8,128)(2,1)} %all-gather.2.cloned.1.call-done, s32[16384]{0:T(1024)S(1)} %broadcast_clamp_fusion), kind=kCustom, calls=%fused_computation | custom fusion | bytes 4259840 | tf_op jit(solution)/shard_map/jit(_take)/gather | solution.py:37
  81.0 3.6 copy.13
  85.1 5.5 collective-permute-start.6
  90.6 4.6 collective-permute-start.5
  95.2 3.1 collective-permute-start.4
  102.6 44.0 %collective-permute-done.6 = bf16[320,4096]{1,0:T(8,128)(2,1)} collective-permute-done((bf16[320,4096]{1,0:T(8,128)(2,1)S(1)}, bf16[320,4096]{1,0:T(8,128)(2,1)}, u32[]{:S(2)}, u32[]{:S(2)}) %collective-permute-start.6) | collective-permute-done | bytes 2621472 | tf_op jit(solution)/shard_map/ppermute | solution.py:13
  146.6 86.0 %collective-permute-start.2 = (bf16[320,4096]{1,0:T(8,128)(2,1)S(1)}, bf16[320,4096]{1,0:T(8,128)(2,1)S(1)}, u32[]{:S(2)}, u32[]{:S(2)}) collective-permute-start(bf16[320,4096]{1,0:T(8,128)(2,1)S(1)} %bitcast.94), channel_id=1, source_target_pairs={{0,4},{2,6},{4,8},{6,10},{8,12},{10,14},{12,16},{14,18},{16,20},{1... | collective-permute-start | bytes 7864328 | tf_op jit(solution)/shard_map/ppermute | solution.py:13
  232.6 55.6 %collective-permute-done.5 = bf16[320,4096]{1,0:T(8,128)(2,1)} collective-permute-done((bf16[320,4096]{1,0:T(8,128)(2,1)S(1)}, bf16[320,4096]{1,0:T(8,128)(2,1)}, u32[]{:S(2)}, u32[]{:S(2)}) %collective-permute-start.5) | collective-permute-done | bytes 2621472 | tf_op jit(solution)/shard_map/ppermute | solution.py:13
  290.0 25.7 %collective-permute-done.4 = bf16[320,4096]{1,0:T(8,128)(2,1)S(1)} collective-permute-done((bf16[320,4096]{1,0:T(8,128)(2,1)S(1)}, bf16[320,4096]{1,0:T(8,128)(2,1)S(1)}, u32[]{:S(2)}, u32[]{:S(2)}) %collective-permute-start.4) | collective-permute-done | bytes 2621472 | tf_op jit(solution)/shard_map/ppermute | solution.py:13
  317.7 90.1 %collective-permute-done.2 = bf16[320,4096]{1,0:T(8,128)(2,1)S(1)} collective-permute-done((bf16[320,4096]{1,0:T(8,128)(2,1)S(1)}, bf16[320,4096]{1,0:T(8,128)(2,1)S(1)}, u32[]{:S(2)}, u32[]{:S(2)}) %collective-permute-start.2) | collective-permute-done | bytes 2621472 | tf_op jit(solution)/shard_map/ppermute | solution.py:13
  410.8 53.9 %collective-permute-done = bf16[320,4096]{1,0:T(8,128)(2,1)} collective-permute-done((bf16[320,4096]{1,0:T(8,128)(2,1)S(1)}, bf16[320,4096]{1,0:T(8,128)(2,1)}, u32[]{:S(2)}, u32[]{:S(2)}) %collective-permute-start) | collective-permute-done | bytes 2621472 | tf_op jit(solution)/shard_map/ppermute | solution.py:13
  464.7 14.5 %multiply_convert_fusion.4 = (bf16[320,4096]{1,0:T(8,128)(2,1)}, bf16[320,4096]{1,0:T(8,128)(2,1)}, bf16[320,4096]{1,0:T(8,128)(2,1)}, bf16[320,4096]{1,0:T(8,12...) fusion(f32[4096]{0:T(1024)S(1)} %copy-done.8, ...), kind=kLoop, calls=%fused_computation.45 | loop fusion | flops 35389440 | bytes 47202304 | tf_op jit(solution)/shard_map/convert_element_type | solution.py:95
  479.2 7.8 %fusion.46 = f32[512,640]{0,1:T(8,128)} fusion(bf16[512,4096]{1,0:T(8,128)(2,1)} %param.7, bf16[320,4096]{1,0:T(8,128)(2,1)} %get-tuple-element.33, bf16[320,4096]{1,0:T(8,128)(2,1)} %copy-done.6), kind=kOutput, calls=%fused_computation.56 | convolution fusion | flops 2694840320 | bytes 10747904 | tf_op jit(solution)/shard_map/dot_general | solution.py:99
  487.3 7.8 %fusion.43 = f32[512,640]{0,1:T(8,128)} fusion(bf16[512,4096]{1,0:T(8,128)(2,1)} %param.7, bf16[320,4096]{1,0:T(8,128)(2,1)} %get-tuple-element.34, bf16[320,4096]{1,0:T(8,128)(2,1)} %collective-permute-done.5), kind=kOutput, calls=%fused_computation.55 | convolution fusion | flops 2694840320 | bytes 10747904 | tf_op jit(solution)/shard_map/dot_general | solution.py:99
  495.1 7.8 %fusion.40 = f32[512,640]{0,1:T(8,128)} fusion(bf16[512,4096]{1,0:T(8,128)(2,1)} %param.7, bf16[320,4096]{1,0:T(8,128)(2,1)} %get-tuple-element.35, bf16[320,4096]{1,0:T(8,128)(2,1)} %collective-permute-done.6), kind=kOutput, calls=%fused_computation.54 | convolution fusion | flops 2694840320 | bytes 10747904 | tf_op jit(solution)/shard_map/dot_general | solution.py:99
  503.0 7.7 %fusion.61 = f32[512,640]{0,1:T(8,128)} fusion(bf16[512,4096]{1,0:T(8,128)(2,1)} %param.7, bf16[320,4096]{1,0:T(8,128)(2,1)} %get-tuple-element.37, bf16[320,4096]{1,0:T(8,128)(2,1)} %collective-permute-done), kind=kOutput, calls=%fused_computation.61 | convolution fusion | flops 2694840320 | bytes 10747904 | tf_op jit(solution)/shard_map/dot_general | solution.py:99
  510.8 7.7 %fusion.58 = f32[512,640]{0,1:T(8,128)} fusion(bf16[512,4096]{1,0:T(8,128)(2,1)} %param.7, bf16[320,4096]{1,0:T(8,128)(2,1)} %get-tuple-element.30, bf16[320,4096]{1,0:T(8,128)(2,1)} %copy-done.5), kind=kOutput, calls=%fused_computation.60 | convolution fusion | flops 2694840320 | bytes 10747904 | tf_op jit(solution)/shard_map/dot_general | solution.py:99
  518.8 7.0 %fusion.49 = f32[512,640]{0,1:T(8,128)} fusion(bf16[512,4096]{1,0:T(8,128)(2,1)} %param.7, bf16[320,4096]{1,0:T(8,128)(2,1)} %get-tuple-element.29, bf16[320,4096]{1,0:T(8,128)(2,1)S(1)} %bitcast.97), kind=kOutput, calls=%fused_computation.57 | convolution fusion | flops 2694840320 | bytes 10747904 | tf_op jit(solution)/shard_map/dot_general | solution.py:99
  525.9 7.7 %fusion.55 = f32[512,640]{0,1:T(8,128)} fusion(bf16[512,4096]{1,0:T(8,128)(2,1)} %param.7, bf16[320,4096]{1,0:T(8,128)(2,1)} %get-tuple-element.31, bf16[320,4096]{1,0:T(8,128)(2,1)} %copy-done.4), kind=kOutput, calls=%fused_computation.59 | convolution fusion | flops 2694840320 | bytes 10747904 | tf_op jit(solution)/shard_map/dot_general | solution.py:99
  533.7 7.9 %fusion.52 = f32[512,640]{0,1:T(8,128)} fusion(bf16[512,4096]{1,0:T(8,128)(2,1)} %param.7, bf16[320,4096]{1,0:T(8,128)(2,1)} %get-tuple-element.32, bf16[320,4096]{1,0:T(8,128)(2,1)} %copy-done.3), kind=kOutput, calls=%fused_computation.58 | convolution fusion | flops 2694840320 | bytes 10747904 | tf_op jit(solution)/shard_map/dot_general | solution.py:99
  541.7 7.0 %fusion.37 = f32[512,640]{0,1:T(8,128)} fusion(bf16[512,4096]{1,0:T(8,128)(2,1)} %param.7, bf16[320,4096]{1,0:T(8,128)(2,1)} %get-tuple-element.36, bf16[320,4096]{1,0:T(8,128)(2,1)S(1)} %copy-done.2), kind=kOutput, calls=%fused_computation.53 | convolution fusion | flops 2694840320 | bytes 10747904 | tf_op jit(solution)/shard_map/dot_general | solution.py:99
  549.1 3.8 fusion
  558.5 12.4 %reduce-scatter.18.cloned.1.call-done = f32[256,640]{0,1:T(8,128)} async-done(((f32[512,640]{0,1:T(8,128)}), f32[256,640]{0,1:T(8,128)}) %reduce-scatter.18.cloned.1.call-update) | async-done | bytes 655376 | tf_op jit(solution)/shard_map/reduce_scatter | solution.py:103
  570.9 15.1 %reduce-scatter.14.cloned.1.call-done = f32[256,640]{0,1:T(8,128)} async-done(((f32[512,640]{0,1:T(8,128)}), f32[256,640]{0,1:T(8,128)}) %reduce-scatter.14.cloned.1.call-update) | async-done | bytes 655376 | tf_op jit(solution)/shard_map/reduce_scatter | solution.py:103
  586.1 15.1 %reduce-scatter.16.cloned.1.call-done = f32[256,640]{0,1:T(8,128)} async-done(((f32[512,640]{0,1:T(8,128)}), f32[256,640]{0,1:T(8,128)}) %reduce-scatter.16.cloned.1.call-update) | async-done | bytes 655376 | tf_op jit(solution)/shard_map/reduce_scatter | solution.py:103
  601.2 15.0 %reduce-scatter.26.cloned.1.call-done = f32[256,640]{0,1:T(8,128)} async-done(((f32[512,640]{0,1:T(8,128)}), f32[256,640]{0,1:T(8,128)}) %reduce-scatter.26.cloned.1.call-update) | async-done | bytes 655376 | tf_op jit(solution)/shard_map/reduce_scatter | solution.py:103
  619.4 3.6 pmax.7
  623.0 4.6 collective-permute-start.8
  629.6 4.3 collective-permute-start.14
  639.7 7.0 %collective-permute-start.11 = (f32[5,64]{1,0:T(8,128)S(1)}, f32[5,64]{1,0:T(8,128)S(1)}, u32[]{:S(2)}, u32[]{:S(2)}) collective-permute-start(f32[5,64]{1,0:T(8,128)S(1)} %get-tuple-element.26), channel_id=1, source_target_pairs={{2,0},{4,2},{6,4},{8,6},{10,8},{12,10},{14,12},{16,14},{18,16},{20... | collective-permute-start | bytes 3848 | tf_op jit(solution)/shard_map/ppermute | solution.py:13
  646.7 3.4 collective-permute-start.10
  (122 shorter events, 39.6 us)
Async XLA Ops:
  6.5 17.7 %all-gather.2.cloned.1.call-start = ((), (), s32[]{:S(2)}) async-start(), calls=%async_computation.9 | async-start | bytes 3145728 | tf_op jit(solution)/shard_map/all_gather | solution.py:53
  8.9 547.2 %reduce-scatter.20.cloned.1.call-start = ((), (), s32[]{:S(2)}) async-start(), calls=%async_computation.15 | async-start | bytes 1966080 | tf_op jit(solution)/shard_map/reduce_scatter | solution.py:103
  84.6 380.1 %copy-start.8 = (f32[4096]{0:T(1024)S(1)}, f32[4096]{0:T(1024)}, u32[]{:S(2)}) copy-start(f32[4096]{0:T(1024)} %param.9) | copy-start | bytes 49156
  85.1 61.5 %collective-permute-start.6 = (bf16[320,4096]{1,0:T(8,128)(2,1)S(1)}, bf16[320,4096]{1,0:T(8,128)(2,1)}, u32[]{:S(2)}, u32[]{:S(2)}) collective-permute-start(bf16[320,4096]{1,0:T(8,128)(2,1)S(1)} %bitcast.89), channel_id=1, source_target_pairs={{6,0},{8,2},{10,4},{12,6},{14,8},{16,10},{18,12},{20,14},{22,16},{... | collective-permute-start | bytes 7864328 | tf_op jit(solution)/shard_map/ppermute | solution.py:13
  90.6 197.5 %collective-permute-start.5 = (bf16[320,4096]{1,0:T(8,128)(2,1)S(1)}, bf16[320,4096]{1,0:T(8,128)(2,1)}, u32[]{:S(2)}, u32[]{:S(2)}) collective-permute-start(bf16[320,4096]{1,0:T(8,128)(2,1)S(1)} %bitcast.90), channel_id=1, source_target_pairs={{4,0},{6,2},{8,4},{10,6},{12,8},{14,10},{16,12},{18,14},{20,16},{2... | collective-permute-start | bytes 7864328 | tf_op jit(solution)/shard_map/ppermute | solution.py:13
  95.2 220.6 %collective-permute-start.4 = (bf16[320,4096]{1,0:T(8,128)(2,1)S(1)}, bf16[320,4096]{1,0:T(8,128)(2,1)S(1)}, u32[]{:S(2)}, u32[]{:S(2)}) collective-permute-start(bf16[320,4096]{1,0:T(8,128)(2,1)S(1)} %bitcast.91), channel_id=1, source_target_pairs={{2,0},{4,2},{6,4},{8,6},{10,8},{12,10},{14,12},{16,14},{18,16},{20... | collective-permute-start | bytes 7864328 | tf_op jit(solution)/shard_map/ppermute | solution.py:13
  98.3 219.4 %collective-permute-start.7 = (bf16[320,4096]{1,0:T(8,128)(2,1)S(1)}, bf16[320,4096]{1,0:T(8,128)(2,1)S(1)}, u32[]{:S(2)}, u32[]{:S(2)}) collective-permute-start(bf16[320,4096]{1,0:T(8,128)(2,1)S(1)} %bitcast.92), channel_id=1, source_target_pairs={{8,0},{10,2},{12,4},{14,6},{16,8},{18,10},{20,12},{22,14},{24,16},... | collective-permute-start | bytes 7864328 | tf_op jit(solution)/shard_map/ppermute | solution.py:13
  100.4 217.3 %collective-permute-start.3 = (bf16[320,4096]{1,0:T(8,128)(2,1)S(1)}, bf16[320,4096]{1,0:T(8,128)(2,1)S(1)}, u32[]{:S(2)}, u32[]{:S(2)}) collective-permute-start(bf16[320,4096]{1,0:T(8,128)(2,1)S(1)} %bitcast.93), channel_id=1, source_target_pairs={{0,2},{2,4},{4,6},{6,8},{8,10},{10,12},{12,14},{14,16},{16,18},{18... | collective-permute-start | bytes 7864328 | tf_op jit(solution)/shard_map/ppermute | solution.py:13
  146.6 261.2 %collective-permute-start.2 = (bf16[320,4096]{1,0:T(8,128)(2,1)S(1)}, bf16[320,4096]{1,0:T(8,128)(2,1)S(1)}, u32[]{:S(2)}, u32[]{:S(2)}) collective-permute-start(bf16[320,4096]{1,0:T(8,128)(2,1)S(1)} %bitcast.94), channel_id=1, source_target_pairs={{0,4},{2,6},{4,8},{6,10},{8,12},{10,14},{12,16},{14,18},{16,20},{1... | collective-permute-start | bytes 7864328 | tf_op jit(solution)/shard_map/ppermute | solution.py:13
  288.1 119.7 %collective-permute-start.1 = (bf16[320,4096]{1,0:T(8,128)(2,1)S(1)}, bf16[320,4096]{1,0:T(8,128)(2,1)S(1)}, u32[]{:S(2)}, u32[]{:S(2)}) collective-permute-start(bf16[320,4096]{1,0:T(8,128)(2,1)S(1)} %bitcast.95), channel_id=1, source_target_pairs={{0,6},{2,8},{4,10},{6,12},{8,14},{10,16},{12,18},{14,20},{16,22},{... | collective-permute-start | bytes 7864328 | tf_op jit(solution)/shard_map/ppermute | solution.py:13
  315.7 92.1 %copy-start.6 = (bf16[320,4096]{1,0:T(8,128)(2,1)}, bf16[320,4096]{1,0:T(8,128)(2,1)S(1)}, u32[]{:S(2)}) copy-start(bf16[320,4096]{1,0:T(8,128)(2,1)S(1)} %collective-permute-done.4) | copy-start | bytes 7864324
  315.7 148.9 %collective-permute-start = (bf16[320,4096]{1,0:T(8,128)(2,1)S(1)}, bf16[320,4096]{1,0:T(8,128)(2,1)}, u32[]{:S(2)}, u32[]{:S(2)}) collective-permute-start(bf16[320,4096]{1,0:T(8,128)(2,1)S(1)} %bitcast.96), channel_id=1, source_target_pairs={{0,8},{2,10},{4,12},{6,14},{8,16},{10,18},{12,20},{14,22},{16,24},... | collective-permute-start | bytes 7864328 | tf_op jit(solution)/shard_map/ppermute | solution.py:13
  317.7 161.5 %copy-start.1 = (bf16[320,4096]{1,0:T(8,128)(2,1)}, bf16[320,4096]{1,0:T(8,128)(2,1)S(1)}, u32[]{:S(2)}) copy-start(bf16[320,4096]{1,0:T(8,128)(2,1)S(1)} %collective-permute-done.7) | copy-start | bytes 7864324
  317.7 90.1 %copy-start.3 = (bf16[320,4096]{1,0:T(8,128)(2,1)}, bf16[320,4096]{1,0:T(8,128)(2,1)S(1)}, u32[]{:S(2)}) copy-start(bf16[320,4096]{1,0:T(8,128)(2,1)S(1)} %collective-permute-done.3) | copy-start | bytes 7864324
  487.0 69.1 %reduce-scatter.22.cloned.1.call-start = ((), (), s32[]{:S(2)}) async-start(), calls=%async_computation.16 | async-start | bytes 1966080 | tf_op jit(solution)/shard_map/reduce_scatter | solution.py:103
  495.1 61.1 %reduce-scatter.24.cloned.1.call-start = ((), (), s32[]{:S(2)}) async-start(), calls=%async_computation.17 | async-start | bytes 1966080 | tf_op jit(solution)/shard_map/reduce_scatter | solution.py:103
  503.0 53.3 %reduce-scatter.10.cloned.1.call-start = ((), (), s32[]{:S(2)}) async-start(), calls=%async_computation.10 | async-start | bytes 1966080 | tf_op jit(solution)/shard_map/reduce_scatter | solution.py:103
  510.8 47.8 %reduce-scatter.12.cloned.1.call-start = ((), (), s32[]{:S(2)}) async-start(), calls=%async_computation.11 | async-start | bytes 1966080 | tf_op jit(solution)/shard_map/reduce_scatter | solution.py:103
  518.6 52.3 %reduce-scatter.18.cloned.1.call-start = ((), (), s32[]{:S(2)}) async-start(), calls=%async_computation.14 | async-start | bytes 1966080 | tf_op jit(solution)/shard_map/reduce_scatter | solution.py:103
  525.8 60.2 %reduce-scatter.14.cloned.1.call-start = ((), (), s32[]{:S(2)}) async-start(), calls=%async_computation.12 | async-start | bytes 1966080 | tf_op jit(solution)/shard_map/reduce_scatter | solution.py:103
  533.6 67.6 %reduce-scatter.16.cloned.1.call-start = ((), (), s32[]{:S(2)}) async-start(), calls=%async_computation.13 | async-start | bytes 1966080 | tf_op jit(solution)/shard_map/reduce_scatter | solution.py:103
  533.7 8.0 %copy-start.2 = (bf16[320,4096]{1,0:T(8,128)(2,1)S(1)}, bf16[320,4096]{1,0:T(8,128)(2,1)}, u32[]{:S(2)}) copy-start(bf16[320,4096]{1,0:T(8,128)(2,1)} %copy-done.1) | copy-start | bytes 7864324
  541.6 74.6 %reduce-scatter.26.cloned.1.call-start = ((), (), s32[]{:S(2)}) async-start(), calls=%async_computation.18 | async-start | bytes 1966080 | tf_op jit(solution)/shard_map/reduce_scatter | solution.py:103
  552.8 81.1 %copy-start = (bf16[64,8192]{0,1:T(8,128)(2,1)S(1)}, bf16[64,8192]{0,1:T(8,128)(2,1)}, u32[]{:S(2)}) copy-start(bf16[64,8192]{0,1:T(8,128)(2,1)} %all-gather.2.cloned.1.call-done) | copy-start | bytes 3145732
  623.0 16.6 %collective-permute-start.8 = (f32[5,64]{1,0:T(8,128)S(1)}, f32[5,64]{1,0:T(8,128)S(1)}, u32[]{:S(2)}, u32[]{:S(2)}) collective-permute-start(f32[5,64]{1,0:T(8,128)S(1)} %get-tuple-element.21), channel_id=1, source_target_pairs={{8,0},{10,2},{12,4},{14,6},{16,8},{18,10},{20,12},{22,14},{24,16},... | collective-permute-start | bytes 3848 | tf_op jit(solution)/shard_map/ppermute | solution.py:13
  627.6 19.1 %collective-permute-start.15 = (f32[5,64]{1,0:T(8,128)S(1)}, f32[5,64]{1,0:T(8,128)S(1)}, u32[]{:S(2)}, u32[]{:S(2)}) collective-permute-start(f32[5,64]{1,0:T(8,128)S(1)} %get-tuple-element.22), channel_id=1, source_target_pairs={{0,8},{2,10},{4,12},{6,14},{8,16},{10,18},{12,20},{14,22},{16,24},... | collective-permute-start | bytes 3848 | tf_op jit(solution)/shard_map/ppermute | solution.py:13
  629.6 20.6 %collective-permute-start.14 = (f32[5,64]{1,0:T(8,128)S(1)}, f32[5,64]{1,0:T(8,128)S(1)}, u32[]{:S(2)}, u32[]{:S(2)}) collective-permute-start(f32[5,64]{1,0:T(8,128)S(1)} %get-tuple-element.23), channel_id=1, source_target_pairs={{0,6},{2,8},{4,10},{6,12},{8,14},{10,16},{12,18},{14,20},{16,22},{... | collective-permute-start | bytes 3848 | tf_op jit(solution)/shard_map/ppermute | solution.py:13
  635.0 17.6 %collective-permute-start.13 = (f32[5,64]{1,0:T(8,128)S(1)}, f32[5,64]{1,0:T(8,128)S(1)}, u32[]{:S(2)}, u32[]{:S(2)}) collective-permute-start(f32[5,64]{1,0:T(8,128)S(1)} %get-tuple-element.24), channel_id=1, source_target_pairs={{0,4},{2,6},{4,8},{6,10},{8,12},{10,14},{12,16},{14,18},{16,20},{1... | collective-permute-start | bytes 3848 | tf_op jit(solution)/shard_map/ppermute | solution.py:13
  637.2 15.5 %collective-permute-start.12 = (f32[5,64]{1,0:T(8,128)S(1)}, f32[5,64]{1,0:T(8,128)S(1)}, u32[]{:S(2)}, u32[]{:S(2)}) collective-permute-start(f32[5,64]{1,0:T(8,128)S(1)} %get-tuple-element.25), channel_id=1, source_target_pairs={{0,2},{2,4},{4,6},{6,8},{8,10},{10,12},{12,14},{14,16},{16,18},{18... | collective-permute-start | bytes 3848 | tf_op jit(solution)/shard_map/ppermute | solution.py:13
  639.7 13.0 %collective-permute-start.11 = (f32[5,64]{1,0:T(8,128)S(1)}, f32[5,64]{1,0:T(8,128)S(1)}, u32[]{:S(2)}, u32[]{:S(2)}) collective-permute-start(f32[5,64]{1,0:T(8,128)S(1)} %get-tuple-element.26), channel_id=1, source_target_pairs={{2,0},{4,2},{6,4},{8,6},{10,8},{12,10},{14,12},{16,14},{18,16},{20... | collective-permute-start | bytes 3848 | tf_op jit(solution)/shard_map/ppermute | solution.py:13
  646.7 5.9 collective-permute-start.10
  650.1 5.6 collective-permute-start.9
  (6 other events, 28.0 us)
Sparse Core Ops, SparseCore 0:
  9.1 15.0 all-gather.1
  487.2 8.4 reduce-scatter.19
  498.1 12.7 reduce-scatter.21
  513.0 12.7 reduce-scatter.23
  528.0 12.7 reduce-scatter.9
  543.0 12.7 reduce-scatter.11
  558.1 12.7 reduce-scatter.17
  573.3 12.7 reduce-scatter.13
  588.4 12.7 reduce-scatter.15
  603.4 12.7 reduce-scatter.25
where the time goes:
time: 667 us; the launch traced here: 663 us
  waiting for transfers between devices  344 us (52%)
  starting transfers between devices  136 us (20%)
  matrix products  68.4 us (10%)
  local copies, waits for them, and re-layouts  66.9 us (10%)
  other arithmetic  27.3 us (4%)
  between operations  14.1 us (2%)
    ppermute x16, waiting for transfers between devices, passed_along(): return lax.ppermute(x, axis, pairs)  272 us
    ppermute x16, starting transfers between devices, passed_along(): return lax.ppermute(x, axis, pairs)  136 us
    dot_general x9, matrix products, product(): lax.dot_general(genotypes, operand, (((1,), (1,)), ((), ())), preferred_e...  68.4 us
    gather x2, local copies, waits for them, and re-layouts, label_rows(): shuffled = jnp.take(whole_rows, shuffles, axis=1)  60.4 us
    reduce_scatter x9, waiting for transfers between devices, shards(): lax.psum_scatter(product(jnp.int32(0), lax.axis_size('sample') * share_ro...  57.7 us
    convert_element_type x1, other arithmetic, shards(): (incoming.astype(jnp.float32) * environment[None, :]).astype(jnp.bfloat16)  14.5 us
    all_gather x1, waiting for transfers between devices, shards(): full_rows = lax.all_gather(phenotypes, 'sample', axis=1, tiled=True)  13.4 us
  transfers between devices with their start and end apart: 26, of which 11 were waited for; matrix products, arithmetic and copies ran while one was open for 11% of the time, Pallas kernels for 0%

commit v1 on v0

v1 whole, which is shorter than its diff:
```python
import functools

import jax
import jax.numpy as jnp
from jax import lax
from jax.experimental import pallas as pl
from jax.experimental.pallas import tpu as pltpu
from jax.sharding import PartitionSpec as P

SNP_BLOCK = 256
MESH = pl.DeviceIdType.MESH
NEAR = (-4, -1, 0, 1, 4)
FAR = (-3, -2, 2, 3)
SLOTS = NEAR + FAR
CORE_SLOTS = (NEAR[:4] + FAR, NEAR[1:] + FAR)
STEP = 512
FAR_STEP = 1024


def window_bounds(window_start, window_end, chrom_bounds, total_blocks):
    middle = (window_start + window_end - 1) // 2
    before = chrom_bounds[None, :] <= middle[:, None]
    lower_edge = jnp.max(jnp.where(before, chrom_bounds[None, :], 0), axis=1)
    upper_edge = jnp.min(jnp.where(before, total_blocks, chrom_bounds[None, :]), axis=1)
    return (jnp.maximum(window_start, lower_edge), jnp.minimum(window_end, upper_edge))


def when(condition, action):
    if condition is None:
        action()
    else:
        pl.when(condition)(action)


def inverse_kernel(own_ref, other_ref, out_ref):
    core = lax.axis_index("sample")
    perms, half = own_ref.shape
    width = 2048
    rows = half // 128
    for p in range(perms):
        total = jnp.zeros((2 * rows, 128), jnp.float32)
        for part, ref in enumerate((own_ref, other_ref)):
            for start in range(0, half, width):
                target = ref[p : p + 1, start : start + width]
                high = (target >> 7) - rows * core
                low = target & 127
                place = lax.broadcasted_iota(jnp.int32, (1, width), 1) + (part * half + start)
                hit = lax.broadcasted_iota(jnp.int32, (rows, width), 0) == high
                place_high = (place >> 7).astype(jnp.float32)
                place_low = (place & 127).astype(jnp.float32)
                left = jnp.concatenate(
                    [jnp.where(hit, place_high, 0.0), jnp.where(hit, place_low, 0.0)], axis=0
                ).astype(jnp.bfloat16)
                right = jnp.where(
                    lax.broadcasted_iota(jnp.int32, (128, width), 0) == low, 1.0, 0.0
                ).astype(jnp.bfloat16)
                total += lax.dot_general(
                    left, right, (((1,), (1,)), ((), ())), preferred_element_type=jnp.float32
                )
        out_ref[p * rows : (p + 1) * rows, :] = (
            total[:rows] * 128.0 + total[rows:]
        ).astype(jnp.int32)


def scan_kernel(
    inv_ref, y_ref, g_ref, env_ref, mask_ref, out_ref,
    h_ref, gp_ref, band_ref, other_ref, env_other, mom_ref, mom_other, reg_ref, div_ref,
    stage0, stage1, near_acc, far_acc, near_in, far_in, peak_ref, msg_ref, msg_in, pow_ref, pow_other,
    y_send, y_recv, g_send, g_recv, s_send, s_recv, p_send, p_recv, m_send, m_recv, local_sem,
):
    me = lax.axis_index("genome")
    core = lax.axis_index("sample")
    indices = lax.axis_size("genome")
    sib = (me, 1 - core)
    genes, half = y_ref.shape
    snps = g_ref.shape[0]

    def inside(o):
        return (me + o >= 0) & (me + o < indices)

    barrier = pltpu.get_barrier_semaphore()
    pl.semaphore_signal(barrier, inc=1, device_id=sib, device_id_type=MESH)
    count = jnp.int32(1)
    for o in SLOTS:
        if o != 0:
            for k in range(2):
                @pl.when(inside(o))
                def _(o=o, k=k):
                    pl.semaphore_signal(barrier, inc=1, device_id=(me + o, k), device_id_type=MESH)
            count = count + jnp.where(inside(o), 2, 0)
    pl.semaphore_wait(barrier, count)

    def remote(src, dst, send, recv, target):
        return pltpu.make_async_remote_copy(
            src, dst, send, recv, device_id=target, device_id_type=MESH
        )

    width = half // 4
    g_copies = [
        remote(
            g_ref.at[:, pl.ds(i * width, width)], other_ref.at[:, pl.ds(i * width, width)],
            g_send.at[i], g_recv.at[i], sib,
        )
        for i in range(4)
    ]
    env_copy = remote(env_ref, env_other, s_send.at[0], s_recv.at[0], sib)
    y_copies = []
    for slot, o in enumerate(SLOTS):
        if o != 0:
            i = len(y_copies)
            y_copies.append((o, remote(
                y_ref, band_ref.at[pl.ds(slot * genes, genes), :], y_send.at[i], y_recv.at[i],
                (me - o, core),
            )))
    own_copy = pltpu.make_async_copy(y_ref, band_ref.at[pl.ds(2 * genes, genes), :], local_sem)
    own_copy.start()
    env_copy.start()
    for copy in g_copies:
        copy.start()
    for o, copy in y_copies:
        when(inside(-o), copy.start)

    lane = lax.broadcasted_iota(jnp.int32, (64, 128), 1)

    def moments(block, _):
        first = pl.multiple_of(block * 64, 64)
        square = jnp.zeros((64, 128), jnp.float32)
        cross = square
        inter = square
        for column in range(half // 128):
            value = g_ref[pl.ds(first, 64), column * 128 : (column + 1) * 128].astype(jnp.float32)
            weight = env_ref[column : column + 1, :]
            value = value * value
            once = value * weight
            square += value
            cross += once
            inter += once * weight
        square = jnp.sum(square, axis=1, keepdims=True)
        cross = jnp.sum(cross, axis=1, keepdims=True)
        inter = jnp.sum(inter, axis=1, keepdims=True)
        mom_ref[pl.ds(first, 64), :] = jnp.where(lane == 0, square, jnp.where(lane == 1, cross, inter))
        return 0

    lax.fori_loop(0, snps // 64, moments, 0)
    mom_copy = remote(mom_ref, mom_other, s_send.at[1], s_recv.at[1], sib)
    mom_copy.start()

    power = jnp.zeros((genes, 128), jnp.float32)
    for column in range(half // 128):
        value = y_ref[:, column * 128 : (column + 1) * 128].astype(jnp.float32)
        power += value * value
    power = jnp.broadcast_to(jnp.sum(power, axis=1, keepdims=True), (genes, 128))
    power = jnp.concatenate([power, power], axis=0)
    pow_ref[...] = jnp.transpose(power)[0:8, :]
    pow_copy = remote(pow_ref, pow_other, s_send.at[2], s_recv.at[2], sib)
    pow_copy.start()

    near_acc[...] = jnp.zeros_like(near_acc)
    far_acc[...] = jnp.zeros_like(far_acc)
    mom_copy.wait_recv()
    env_copy.wait_recv()
    for q in range(4):
        rows = slice(q * 128, (q + 1) * 128)
        total = mom_ref[rows, :] + mom_other[rows, :]
        square, cross, inter = total[:, 0:1], total[:, 1:2], total[:, 2:3]
        regression = cross / square
        divisor = inter - cross * regression + 0.1 * inter
        reg_ref[rows, :] = jnp.broadcast_to(regression, (128, 128))
        div_ref[:, rows] = jnp.transpose(jnp.broadcast_to(divisor, (128, 128)))[0:8, :]

    def residuals(source, weights, first, chunk):
        for s in range(2):
            start = pl.multiple_of(chunk * 256 + s * 128, 128)
            weight = weights[pl.ds(chunk * 2 + s, 1), :]
            for q in range(4):
                rows = slice(q * 128, (q + 1) * 128)
                value = source[rows, pl.ds(start, 128)].astype(jnp.float32)
                value = jnp.transpose(value * (weight - reg_ref[rows, :]))
                h_ref[pl.ds(first + start, 128), q, :] = value

    def own_residuals(chunk, _):
        residuals(g_ref, env_ref, 0, chunk)
        return 0

    lax.fori_loop(0, half // 256, own_residuals, 0)
    own_copy.wait()
    for o, copy in y_copies:
        if o in NEAR:
            when(inside(o), copy.wait_recv)

    def right_side(ref, first, b, count):
        return jnp.concatenate(
            [ref[pl.ds(first, count), 2 * b + i, :] for i in range(2)], axis=1
        ).astype(jnp.bfloat16)

    def near_product(label, k, sides):
        for b in range(2):
            left = band_ref[64 * b : 64 * b + 256, pl.ds(pl.multiple_of(k * STEP, STEP), STEP)]
            near_acc[2 * label + b] += jnp.dot(left, sides[b], preferred_element_type=jnp.float32)

    def plain(k, _):
        near_product(0, k, [right_side(h_ref, pl.multiple_of(k * STEP, STEP), b, STEP) for b in range(2)])
        return 0

    lax.fori_loop(0, half // STEP, plain, 0)

    for i in range(4):
        g_copies[i].wait_recv()

        def other_residuals(chunk, _):
            residuals(other_ref, env_other, half, chunk)
            return 0

        lax.fori_loop(i * width // 256, (i + 1) * width // 256, other_residuals, 0)

    per_label = half // STEP
    steps = 4 * per_label

    def gather(stage, n):
        base = n * STEP
        for t in range(STEP):
            stage[t] = h_ref[inv_ref[base + t]]

    def consume(stage, n):
        sides = [right_side(stage, 0, b, STEP) for b in range(2)]
        for b in range(2):
            gp_ref[pl.ds(pl.multiple_of(n * STEP, STEP), STEP), 256 * b : 256 * b + 256] = sides[b]
        near_product(1 + lax.div(n, per_label), lax.rem(n, per_label), sides)

    def permuted(i, _):
        n = 2 * i
        gather(stage1, n + 1)
        consume(stage0, n)
        gather(stage0, lax.rem(n + 2, steps))
        consume(stage1, n + 1)
        return 0

    gather(stage0, 0)
    lax.fori_loop(0, steps // 2, permuted, 0)

    partials = []
    for label in range(5):
        copy = remote(
            near_acc.at[2 * label + 1 - core], near_in.at[label], p_send.at[label], p_recv.at[label], sib
        )
        copy.start()
        partials.append(copy)
    for o, copy in y_copies:
        if o in FAR:
            when(inside(o), copy.wait_recv)

    for label in range(5):
        def distant(k, _, label=label):
            start = pl.multiple_of(k * FAR_STEP, FAR_STEP)
            left = band_ref[320:576, pl.ds(start, FAR_STEP)]
            for b in range(2):
                if label == 0:
                    side = right_side(h_ref, start, b, FAR_STEP)
                else:
                    side = gp_ref[pl.ds(start + (label - 1) * half, FAR_STEP), 256 * b : 256 * b + 256]
                far_acc[2 * label + b] += jnp.dot(left, side, preferred_element_type=jnp.float32)
            return 0

        lax.fori_loop(0, half // FAR_STEP, distant, 0)
        copy = remote(
            far_acc.at[2 * label + 1 - core], far_in.at[label], p_send.at[5 + label], p_recv.at[5 + label], sib
        )
        copy.start()
        partials.append(copy)

    divisor = div_ref[0:1, pl.ds(pl.multiple_of(core * 256, 256), 256)]
    lanes = lax.broadcasted_iota(jnp.int32, (256, 128), 1)
    for part, (acc, arrived) in enumerate(((near_acc, near_in), (far_acc, far_in))):
        peaks = jnp.zeros((256, 128), jnp.float32)
        for label in range(5):
            partials[5 * part + label].wait_recv()
            numerator = acc[2 * label + core] + arrived[label]
            scores = numerator * numerator / divisor
            peaks = jnp.where(lanes == label, jnp.max(scores, axis=1, keepdims=True), peaks)
        peak_ref[:, 256 * part : 256 * part + 128] = jnp.transpose(peaks[0:128])[0:8, :]
        peak_ref[:, 256 * part + 128 : 256 * part + 256] = jnp.transpose(peaks[128:256])[0:8, :]
    found = jnp.where(mask_ref[0:1, :] > 0.0, peak_ref[...], 0.0)
    msg_ref[...] = jnp.zeros_like(msg_ref)
    for s in range(8):
        msg_ref[s, :, 0:64] = found[:, 64 * s : 64 * s + 64]

    sends = []
    for c in range(2):
        for s, o in enumerate(CORE_SLOTS[c]):
            for k in range(2):
                if o == 0 and k == c:
                    continue
                copy = remote(
                    msg_ref.at[s], msg_in.at[2 * SLOTS.index(o) + c], m_send.at[2 * s + k],
                    m_recv.at[2 * SLOTS.index(o) + c], (me + o, k),
                )
                condition = (core == c) if o == 0 else (core == c) & inside(o)
                when(condition, copy.start)
                sends.append((condition, copy))

    best = jnp.where(core == 0, msg_ref[2], msg_ref[1])
    for c in range(2):
        for o in CORE_SLOTS[c]:
            index = 2 * SLOTS.index(o) + c
            condition = (core == 1 - c) if o == 0 else inside(-o)
            copy = remote(msg_ref.at[0], msg_in.at[index], m_send.at[0], m_recv.at[index], sib)
            when(condition, copy.wait_recv)
            best = jnp.maximum(best, jnp.where(condition, msg_in[index], 0.0))
    pow_copy.wait_recv()
    power = pow_ref[...] + pow_other[...]
    result = jnp.sqrt(best / (power / (2.0 * half) + 1e-05))
    out_ref[...] = result[0:5, 0:64]

    for copy in g_copies + [env_copy, mom_copy, pow_copy] + partials:
        copy.wait_send()
    for o, copy in y_copies:
        when(inside(-o), copy.wait_send)
    for condition, copy in sends:
        when(condition, copy.wait_send)


def shards(genotypes, phenotypes, environment, shuffles, window_start, window_end, chrom_bounds):
    snps, half = genotypes.shape
    genes = phenotypes.shape[0]
    labels = shuffles.shape[0] + 1
    genome_size = lax.axis_size("genome")
    me = lax.axis_index("genome")
    core = lax.axis_index("sample")
    vmem = pl.BlockSpec(memory_space=pltpu.VMEM)

    shuffles_other = lax.ppermute(shuffles, "sample", [(0, 1), (1, 0)])
    inverse = pl.pallas_call(
        inverse_kernel,
        name="invert",
        out_shape=jax.ShapeDtypeStruct(((labels - 1) * half // 128, 128), jnp.int32),
        in_specs=[vmem, vmem],
        out_specs=vmem,
    )(shuffles, shuffles_other)

    total_blocks = snps * genome_size // SNP_BLOCK
    lower_edge, upper_edge = window_bounds(window_start, window_end, chrom_bounds, total_blocks)
    padding = jnp.zeros((4 * genes,), jnp.int32)
    edges = jnp.stack([
        jnp.concatenate([padding, lower_edge, padding]),
        jnp.concatenate([padding, upper_edge, padding]),
    ])
    band = lax.dynamic_slice_in_dim(edges, me * genes, 9 * genes, 1).reshape(2, 9, genes)
    block = me * (snps // SNP_BLOCK) + core
    hits = ((band[0] <= block) & (block < band[1])).astype(jnp.float32)
    masks = [
        jnp.concatenate([hits[o + 4] for o in CORE_SLOTS[c]]).reshape(1, 8 * genes) for c in range(2)
    ]
    mask = jnp.broadcast_to(jnp.where(core == 0, masks[0], masks[1]), (8, 8 * genes))

    f32, bf16 = jnp.float32, jnp.bfloat16
    dma = pltpu.SemaphoreType.DMA
    return pl.pallas_call(
        scan_kernel,
        name="scan",
        out_shape=jax.ShapeDtypeStruct((labels, genes), jnp.float32),
        in_specs=[pl.BlockSpec(memory_space=pltpu.SMEM), vmem, vmem, vmem, vmem],
        out_specs=vmem,
        scratch_shapes=[
            pltpu.VMEM((2 * half, 4, 128), f32),
            pltpu.VMEM((4 * half, snps), bf16),
            pltpu.VMEM((9 * genes, half), bf16),
            pltpu.VMEM((snps, half), bf16),
            pltpu.VMEM((half // 128, 128), f32),
            pltpu.VMEM((snps, 128), f32),
            pltpu.VMEM((snps, 128), f32),
            pltpu.VMEM((snps, 128), f32),
            pltpu.VMEM((8, snps), f32),
            pltpu.VMEM((STEP, 4, 128), f32),
            pltpu.VMEM((STEP, 4, 128), f32),
            pltpu.VMEM((2 * labels, 256, 256), f32),
            pltpu.VMEM((2 * labels, 256, 256), f32),
            pltpu.VMEM((labels, 256, 256), f32),
            pltpu.VMEM((labels, 256, 256), f32),
            pltpu.VMEM((8, 8 * genes), f32),
            pltpu.VMEM((8, 8, 128), f32),
            pltpu.VMEM((18, 8, 128), f32),
            pltpu.VMEM((8, 128), f32),
            pltpu.VMEM((8, 128), f32),
            dma((8,)), dma((8,)), dma((4,)), dma((4,)), dma((3,)), dma((3,)),
            dma((10,)), dma((10,)), dma((16,)), dma((18,)), dma(()),
        ],
        compiler_params=pltpu.CompilerParams(
            collective_id=0, has_side_effects=True, vmem_limit_bytes=64 * 1024 * 1024 - 65536
        ),
    )(inverse.reshape(-1), phenotypes, genotypes, environment.reshape(-1, 128), mask)


def solution(mesh):
    placed = (
        P("genome", "sample"),
        P("genome", "sample"),
        P("sample"),
        P(None, "sample"),
        P(),
        P(),
        P(),
    )
    return jax.shard_map(
        shards, mesh=mesh, in_specs=placed, out_specs=P(None, "genome"), check_vma=False
    )
```

time: 667 us -> 133 us (0.20)
  waiting for transfers between devices: 344 us -> 0.01 us
  starting transfers between devices: 136 us -> 0.68 us
  Pallas kernels: 0 us -> 126 us
  matrix products: 68.4 us -> 0 us
  local copies, waits for them, and re-layouts: 66.9 us -> 2.75 us
  other arithmetic: 27.3 us -> 3.21 us
  between operations: 14.1 us -> 0.06 us
    ppermute x16 -> x1, waiting for transfers between devices: 272 us -> 0.01 us  [shards(): shuffles_other = lax.ppermute(shuffles, 'sample', [(0, 1), (1, 0)])]
    ppermute x16 -> x1, starting transfers between devices: 136 us -> 0.68 us  [shards(): shuffles_other = lax.ppermute(shuffles, 'sample', [(0, 1), (1, 0)])]
    pallas_call x0 -> x2, Pallas kernels: none -> 126 us  [the longest x1 121 us: shards(): pl.pallas_call(scan_kernel, name='scan', out_shape=jax.ShapeDtypeStruct((...]
    dot_general x9 -> x0, matrix products: 68.4 us -> none  [product(): lax.dot_general(genotypes, operand, (((1,), (1,)), ((), ())), preferred_e...]
    gather x2 -> x0, local copies, waits for them, and re-layouts: 60.4 us -> none  [label_rows(): shuffled = jnp.take(whole_rows, shuffles, axis=1)]
    reduce_scatter x9 -> x0, waiting for transfers between devices: 57.7 us -> none  [shards(): lax.psum_scatter(product(jnp.int32(0), lax.axis_size('sample') * share_ro...]
    convert_element_type x1, other arithmetic: 14.5 us -> 0.01 us  [shards(): hits = ((band[0] <= block) & (block < band[1])).astype(jnp.float32)]
    all_gather x1 -> x0, waiting for transfers between devices: 13.4 us -> none  [shards(): full_rows = lax.all_gather(phenotypes, 'sample', axis=1, tiled=True)]
  transfers between devices with their start and end apart: 26 -> 1, of which waited for: 11 -> 0; matrix products, arithmetic and copies ran while one was open for 11% -> 3% of each run, Pallas kernels for 0% -> 0%
where the time goes in v1:
time: 133 us; the launch traced here: 132 us
  Pallas kernels  126 us (95%)
  other arithmetic  3.21 us (2%)
  local copies, waits for them, and re-layouts  2.75 us (2%)
    pallas_call x1, Pallas kernels, shards(): pl.pallas_call(scan_kernel, name='scan', out_shape=jax.ShapeDtypeStruct((...  121 us
    pallas_call x1, Pallas kernels, shards(): pl.pallas_call(inverse_kernel, name='invert', out_shape=jax.ShapeDtypeStr...  4.53 us
  transfers between devices with their start and end apart: 1, of which 0 were waited for; matrix products, arithmetic and copies ran while one was open for 3% of the time, Pallas kernels for 0%

profile of v1, /device:TPU:97, one launch (start us, length us, event | category | flops | bytes accessed | tf_op | source)
XLA Modules:
  0.0 132.2 jit_solution(14917589832330140347)
XLA Ops:
  0.0 0.7 collective-permute-start
  0.7 0.7 add_select_fusion
  1.4 0.9 fusion.1
  2.3 0.7 min.3
  3.1 0.7 max.3
  3.9 0.1 fusion.4
  3.9 0.1 slice_bitcast_fusion
  4.0 0.1 concatenate.48
  4.1 0.1 concatenate.50
  4.2 0.0 collective-permute-done.other_ref
  4.2 0.0 copy-start
  4.2 0.6 copy-done
  4.8 4.5 %invert.1 = s32[128,128]{1,0:T(8,128)} custom-call(s32[4,4096]{1,0:T(4,128)} %own_ref.1, s32[4,4096]{1,0:T(4,128)} %copy-done), custom_call_target="tpu_custom_call" | custom-call | tf_op jit(solution)/shard_map/invert/pallas_call | solution.py:332
  9.3 0.6 broadcast_in_dim.35.mask_ref
  9.9 121.0 %scan.1 = f32[5,64]{1,0:T(8,128)} custom-call(s32[16384]{0:T(1024)} %bitcast.20, bf16[64,4096]{1,0:T(8,128)(2,1)} %y_ref.1, bf16[512,4096]{1,0:T(8,128)(2,1)} %g_ref.1, f32[32,128]{1,0:T(8,128)} %bitcast.21, f32[8,512]{1,0:T(8,128)} %broadcast_in_dim.35.mask_ref), custom_call_target="tpu_custom_call" | custom-call | tf_op jit(solution)/shard_map/scan/pallas_call | solution.py:357
  130.9 1.3 copy.9
  (6 shorter events, 0.1 us)
Async XLA Ops:
  0.0 4.2 %collective-permute-start = (s32[4,4096]{1,0:T(4,128)}, s32[4,4096]{1,0:T(4,128)S(1)}, u32[]{:S(2)}, u32[]{:S(2)}) collective-permute-start(s32[4,4096]{1,0:T(4,128)} %own_ref.1), channel_id=1, source_target_pairs={{0,1},{1,0},{2,3},{3,2},{4,5},{5,4},{6,7},{7,6},{8,9},{9,8},{10,11... | collective-permute-start | bytes 196616 | tf_op jit(solution)/shard_map/ppermute | solution.py:331
  4.2 0.6 copy-start

commit v2 on v1

--- a/solution.py
+++ b/solution.py
@@ -9,20 +9,16 @@
 
 SNP_BLOCK = 256
 MESH = pl.DeviceIdType.MESH
-NEAR = (-4, -1, 0, 1, 4)
-FAR = (-3, -2, 2, 3)
-SLOTS = NEAR + FAR
-CORE_SLOTS = (NEAR[:4] + FAR, NEAR[1:] + FAR)
+SLOTS = (
+    (-4, 3, 0, 1, 4, 2, -3, -2, -1),
+    (-4, -1, 0, 1, 4, 2, -3, 3, -2),
+    (-4, -1, 0, 1, 4, -2, -3, 3, 2),
+    (-4, -1, 0, -3, 4, -2, 3, 2, 1),
+)
+CORE_SLOTS = ((0, 1, 2, 3, 5, 6, 7, 8), (1, 2, 3, 4, 5, 6, 7, 8))
 STEP = 512
 FAR_STEP = 1024
-
-
-def window_bounds(window_start, window_end, chrom_bounds, total_blocks):
-    middle = (window_start + window_end - 1) // 2
-    before = chrom_bounds[None, :] <= middle[:, None]
-    lower_edge = jnp.max(jnp.where(before, chrom_bounds[None, :], 0), axis=1)
-    upper_edge = jnp.min(jnp.where(before, total_blocks, chrom_bounds[None, :]), axis=1)
-    return (jnp.maximum(window_start, lower_edge), jnp.minimum(window_end, upper_edge))
+SPLIT = 2
 
 
 def when(condition, action):
@@ -59,11 +55,11 @@
                 )
         out_ref[p * rows : (p + 1) * rows, :] = (
             total[:rows] * 128.0 + total[rows:]
-        ).astype(jnp.int32)
+        ).astype(jnp.int32) * 4
 
 
 def scan_kernel(
-    inv_ref, y_ref, g_ref, env_ref, mask_ref, out_ref,
+    inv_ref, bounds_ref, y_ref, g_ref, env_ref, start_ref, end_ref, out_ref,
     h_ref, gp_ref, band_ref, other_ref, env_other, mom_ref, mom_other, reg_ref, div_ref,
     stage0, stage1, near_acc, far_acc, near_in, far_in, peak_ref, msg_ref, msg_in, pow_ref, pow_other,
     y_send, y_recv, g_send, g_recv, s_send, s_recv, p_send, p_recv, m_send, m_recv, local_sem,
@@ -81,7 +77,7 @@
     barrier = pltpu.get_barrier_semaphore()
     pl.semaphore_signal(barrier, inc=1, device_id=sib, device_id_type=MESH)
     count = jnp.int32(1)
-    for o in SLOTS:
+    for o in range(-4, 5):
         if o != 0:
             for k in range(2):
                 @pl.when(inside(o))
@@ -104,21 +100,151 @@
         for i in range(4)
     ]
     env_copy = remote(env_ref, env_other, s_send.at[0], s_recv.at[0], sib)
-    y_copies = []
-    for slot, o in enumerate(SLOTS):
-        if o != 0:
-            i = len(y_copies)
-            y_copies.append((o, remote(
-                y_ref, band_ref.at[pl.ds(slot * genes, genes), :], y_send.at[i], y_recv.at[i],
-                (me - o, core),
-            )))
+    place = lax.rem(me, 4)
+    line = lax.div(me, 4)
+    piece = genes // 2
+    above, below = line > 0, line < indices // 4 - 1
+    hops = []
+
+    def slot_valid(slot):
+        checks = []
+        for x in range(4):
+            o = SLOTS[x][slot]
+            if not 0 <= x + o < 4:
+                checks.append((place == x, above if x + o < 0 else below))
+        return checks
+
+    def slot_wait(slot, part):
+        copy = remote(
+            y_ref.at[pl.ds(0, piece), :], band_ref.at[pl.ds(slot * genes + part * piece, piece), :],
+            y_send.at[0], y_recv.at[2 * slot + part], sib,
+        )
+        bad = None
+        for at, exists in slot_valid(slot):
+            term = at & jnp.logical_not(exists)
+            bad = term if bad is None else bad | term
+        when(None if bad is None else jnp.logical_not(bad), copy.wait_recv)
+
+    def hop(x, link, shift, part):
+        step = {"right": 1, "left": -1, "up": -4, "down": 4}[link]
+        needs = set()
+        if link in ("right", "left"):
+            other = (x + step) % 4
+            step = other - x
+        else:
+            other = x
+            needs.add(link)
+        if not 0 <= x + shift < 4:
+            needs.add("up" if x + shift < 0 else "down")
+        here = SLOTS[x].index(shift)
+        there = SLOTS[other].index(shift - step)
+        index = sum(1 for at, _ in hops if at == x)
+        if shift == 0:
+            source = y_ref.at[pl.ds(part * piece, piece), :]
+        else:
+            source = band_ref.at[pl.ds(here * genes + part * piece, piece), :]
+        copy = remote(
+            source, band_ref.at[pl.ds(there * genes + part * piece, piece), :],
+            y_send.at[index], y_recv.at[2 * there + part], (me + step, core),
+        )
+        when(rows_exist(needs), copy.start)
+        hops.append((x, needs))
+
+    def rows_exist(needs):
+        if needs == {"up", "down"}:
+            return above & below
+        return {"up": above, "down": below}[min(needs)] if needs else None
+
+    def finish_hops():
+        for x in range(4):
+            @pl.when(place == x)
+            def _(x=x):
+                for index, needs in enumerate([needs for at, needs in hops if at == x]):
+                    copy = remote(
+                        y_ref.at[pl.ds(0, piece), :], band_ref.at[pl.ds(0, piece), :],
+                        y_send.at[index], y_recv.at[0], sib,
+                    )
+                    when(rows_exist(needs), copy.wait_send)
+
+    def first_hops():
+        for x in range(4):
+            @pl.when(place == x)
+            def _(x=x):
+                for part in range(2):
+                    for link in ("right", "left", "down", "up"):
+                        hop(x, link, 0, part)
+
+    def second_hops():
+        for slot in (1, 3, 0, 4):
+            for part in range(2):
+                slot_wait(slot, part)
+        for x in range(4):
+            @pl.when(place == x)
+            def _(x=x):
+                left, right = SLOTS[x][1], SLOTS[x][3]
+                hop(x, "right", left, 1)
+                hop(x, "left", right, 0)
+                if x < 3:
+                    for part in ((0, 1) if x == 0 else (1, 0)):
+                        hop(x, "down", right, part)
+                if x > 0:
+                    for part in ((1, 0) if x == 3 else (0, 1)):
+                        hop(x, "up", left, part)
+                if x == 3:
+                    hop(x, "right", -4, 0)
+                    hop(x, "right", -4, 1)
+                if x == 0:
+                    hop(x, "left", 4, 0)
+                    hop(x, "left", 4, 1)
+
+    def third_hops():
+        for part in range(2):
+            slot_wait(5, part)
+        for x in range(4):
+            @pl.when(place == x)
+            def _(x=x):
+                if x == 0:
+                    hop(x, "down", 2, 0)
+                if x == 1:
+                    hop(x, "down", 2, 0)
+                if x == 2:
+                    hop(x, "up", -2, 1)
+                if x == 3:
+                    hop(x, "up", -2, 1)
+        middle = (place == 1) | (place == 2)
+        for slot, part, exists in ((6, 1, above), (7, 0, below)):
+            copy = remote(
+                y_ref.at[pl.ds(0, piece), :], band_ref.at[pl.ds(slot * genes + part * piece, piece), :],
+                y_send.at[0], y_recv.at[2 * slot + part], sib,
+            )
+            pl.when(middle & exists)(copy.wait_recv)
+        for x in (1, 2):
+            @pl.when(place == x)
+            def _(x=x):
+                hop(x, "left", -3, 1)
+                hop(x, "right", 3, 0)
+
+    def last_arrivals():
+        for slot in (6, 7, 8):
+            for part in range(2):
+                early = {(6, 1): True, (7, 0): True}.get((slot, part), False)
+                copy = remote(
+                    y_ref.at[pl.ds(0, piece), :], band_ref.at[pl.ds(slot * genes + part * piece, piece), :],
+                    y_send.at[0], y_recv.at[2 * slot + part], sib,
+                )
+                for x in range(4):
+                    if early and x in (1, 2):
+                        continue
+                    o = SLOTS[x][slot]
+                    exists = above if x + o < 0 else below
+                    pl.when((place == x) & exists)(copy.wait_recv)
+
     own_copy = pltpu.make_async_copy(y_ref, band_ref.at[pl.ds(2 * genes, genes), :], local_sem)
     own_copy.start()
     env_copy.start()
     for copy in g_copies:
         copy.start()
-    for o, copy in y_copies:
-        when(inside(-o), copy.start)
+    first_hops()
 
     lane = lax.broadcasted_iota(jnp.int32, (64, 128), 1)
 
@@ -176,7 +302,7 @@
                 rows = slice(q * 128, (q + 1) * 128)
                 value = source[rows, pl.ds(start, 128)].astype(jnp.float32)
                 value = jnp.transpose(value * (weight - reg_ref[rows, :]))
-                h_ref[pl.ds(first + start, 128), q, :] = value
+                h_ref[pl.ds((first + start) * 4 + q, 128, stride=4), :] = value
 
     def own_residuals(chunk, _):
         residuals(g_ref, env_ref, 0, chunk)
@@ -184,13 +310,11 @@
 
     lax.fori_loop(0, half // 256, own_residuals, 0)
     own_copy.wait()
-    for o, copy in y_copies:
-        if o in NEAR:
-            when(inside(o), copy.wait_recv)
+    second_hops()
 
     def right_side(ref, first, b, count):
         return jnp.concatenate(
-            [ref[pl.ds(first, count), 2 * b + i, :] for i in range(2)], axis=1
+            [ref[pl.ds(first + 2 * b + i, count, stride=4), :] for i in range(2)], axis=1
         ).astype(jnp.bfloat16)
 
     def near_product(label, k, sides):
@@ -199,7 +323,7 @@
             near_acc[2 * label + b] += jnp.dot(left, sides[b], preferred_element_type=jnp.float32)
 
     def plain(k, _):
-        near_product(0, k, [right_side(h_ref, pl.multiple_of(k * STEP, STEP), b, STEP) for b in range(2)])
+        near_product(0, k, [right_side(h_ref, k * (4 * STEP), b, STEP) for b in range(2)])
         return 0
 
     lax.fori_loop(0, half // STEP, plain, 0)
@@ -219,7 +343,7 @@
     def gather(stage, n):
         base = n * STEP
         for t in range(STEP):
-            stage[t] = h_ref[inv_ref[base + t]]
+            stage[4 * t : 4 * t + 4, :] = h_ref[pl.ds(inv_ref[base + t], 4), :]
 
     def consume(stage, n):
         sides = [right_side(stage, 0, b, STEP) for b in range(2)]
@@ -236,7 +360,9 @@
         return 0
 
     gather(stage0, 0)
-    lax.fori_loop(0, steps // 2, permuted, 0)
+    lax.fori_loop(0, SPLIT, permuted, 0)
+    third_hops()
+    lax.fori_loop(SPLIT, steps // 2, permuted, 0)
 
     partials = []
     for label in range(5):
@@ -245,9 +371,7 @@
         )
         copy.start()
         partials.append(copy)
-    for o, copy in y_copies:
-        if o in FAR:
-            when(inside(o), copy.wait_recv)
+    last_arrivals()
 
     for label in range(5):
         def distant(k, _, label=label):
@@ -255,7 +379,7 @@
             left = band_ref[320:576, pl.ds(start, FAR_STEP)]
             for b in range(2):
                 if label == 0:
-                    side = right_side(h_ref, start, b, FAR_STEP)
+                    side = right_side(h_ref, k * (4 * FAR_STEP), b, FAR_STEP)
                 else:
                     side = gp_ref[pl.ds(start + (label - 1) * half, FAR_STEP), 256 * b : 256 * b + 256]
                 far_acc[2 * label + b] += jnp.dot(left, side, preferred_element_type=jnp.float32)
@@ -279,29 +403,49 @@
             peaks = jnp.where(lanes == label, jnp.max(scores, axis=1, keepdims=True), peaks)
         peak_ref[:, 256 * part : 256 * part + 128] = jnp.transpose(peaks[0:128])[0:8, :]
         peak_ref[:, 256 * part + 128 : 256 * part + 256] = jnp.transpose(peaks[128:256])[0:8, :]
-    found = jnp.where(mask_ref[0:1, :] > 0.0, peak_ref[...], 0.0)
     msg_ref[...] = jnp.zeros_like(msg_ref)
+    shifts = [sum(jnp.where(place == x, SLOTS[x][slot], 0) for x in range(4)) for slot in range(9)]
+    block = me * (snps // SNP_BLOCK) + core
+    total_blocks = indices * (snps // SNP_BLOCK)
     for s in range(8):
-        msg_ref[s, :, 0:64] = found[:, 64 * s : 64 * s + 64]
+        shift = jnp.where(core == 0, shifts[CORE_SLOTS[0][s]], shifts[CORE_SLOTS[1][s]])
+        owner = jnp.clip(me + shift, 0, indices - 1)
+        odd = lax.rem(owner, 2) == 1
+        begin = start_ref[pl.ds(lax.div(owner, 2), 1), :]
+        finish = end_ref[pl.ds(lax.div(owner, 2), 1), :]
+        begin = jnp.where(odd, begin[:, 64:128], begin[:, 0:64])
+        finish = jnp.where(odd, finish[:, 64:128], finish[:, 0:64])
+        middle = (begin + finish - 1) >> 1
+        lower = jnp.zeros_like(middle)
+        upper = jnp.full_like(middle, total_blocks)
+        for k in range(bounds_ref.shape[0]):
+            bound = bounds_ref[k]
+            before = bound <= middle
+            lower = jnp.maximum(lower, jnp.where(before, bound, 0))
+            upper = jnp.minimum(upper, jnp.where(before, total_blocks, bound))
+        inner = (jnp.maximum(begin, lower) <= block) & (block < jnp.minimum(finish, upper))
+        msg_ref[s, :, 0:64] = jnp.where(inner, peak_ref[:, 64 * s : 64 * s + 64], 0.0)
 
     sends = []
     for c in range(2):
-        for s, o in enumerate(CORE_SLOTS[c]):
+        for s in range(8):
             for k in range(2):
-                if o == 0 and k == c:
+                local = CORE_SLOTS[c][s] == 2
+                if local and k == c:
                     continue
+                shift = shifts[CORE_SLOTS[c][s]]
                 copy = remote(
-                    msg_ref.at[s], msg_in.at[2 * SLOTS.index(o) + c], m_send.at[2 * s + k],
-                    m_recv.at[2 * SLOTS.index(o) + c], (me + o, k),
+                    msg_ref.at[s], msg_in.at[2 * (shift + 4) + c], m_send.at[2 * s + k],
+                    m_recv.at[2 * (shift + 4) + c], (me + shift, k),
                 )
-                condition = (core == c) if o == 0 else (core == c) & inside(o)
+                condition = (core == c) & inside(shift)
                 when(condition, copy.start)
                 sends.append((condition, copy))
 
     best = jnp.where(core == 0, msg_ref[2], msg_ref[1])
     for c in range(2):
-        for o in CORE_SLOTS[c]:
-            index = 2 * SLOTS.index(o) + c
+        for o in range(-4 + c, 4 + c):
+            index = 2 * (o + 4) + c
             condition = (core == 1 - c) if o == 0 else inside(-o)
             copy = remote(msg_ref.at[0], msg_in.at[index], m_send.at[0], m_recv.at[index], sib)
             when(condition, copy.wait_recv)
@@ -313,8 +457,7 @@
 
     for copy in g_copies + [env_copy, mom_copy, pow_copy] + partials:
         copy.wait_send()
-    for o, copy in y_copies:
-        when(inside(-o), copy.wait_send)
+    finish_hops()
     for condition, copy in sends:
         when(condition, copy.wait_send)
 
@@ -323,9 +466,6 @@
     snps, half = genotypes.shape
     genes = phenotypes.shape[0]
     labels = shuffles.shape[0] + 1
-    genome_size = lax.axis_size("genome")
-    me = lax.axis_index("genome")
-    core = lax.axis_index("sample")
     vmem = pl.BlockSpec(memory_space=pltpu.VMEM)
 
     shuffles_other = lax.ppermute(shuffles, "sample", [(0, 1), (1, 0)])
@@ -337,31 +477,16 @@
         out_specs=vmem,
     )(shuffles, shuffles_other)
 
-    total_blocks = snps * genome_size // SNP_BLOCK
-    lower_edge, upper_edge = window_bounds(window_start, window_end, chrom_bounds, total_blocks)
-    padding = jnp.zeros((4 * genes,), jnp.int32)
-    edges = jnp.stack([
-        jnp.concatenate([padding, lower_edge, padding]),
-        jnp.concatenate([padding, upper_edge, padding]),
-    ])
-    band = lax.dynamic_slice_in_dim(edges, me * genes, 9 * genes, 1).reshape(2, 9, genes)
-    block = me * (snps // SNP_BLOCK) + core
-    hits = ((band[0] <= block) & (block < band[1])).astype(jnp.float32)
-    masks = [
-        jnp.concatenate([hits[o + 4] for o in CORE_SLOTS[c]]).reshape(1, 8 * genes) for c in range(2)
-    ]
-    mask = jnp.broadcast_to(jnp.where(core == 0, masks[0], masks[1]), (8, 8 * genes))
-
     f32, bf16 = jnp.float32, jnp.bfloat16
     dma = pltpu.SemaphoreType.DMA
     return pl.pallas_call(
         scan_kernel,
         name="scan",
         out_shape=jax.ShapeDtypeStruct((labels, genes), jnp.float32),
-        in_specs=[pl.BlockSpec(memory_space=pltpu.SMEM), vmem, vmem, vmem, vmem],
+        in_specs=[pl.BlockSpec(memory_space=pltpu.SMEM)] * 2 + [vmem] * 5,
         out_specs=vmem,
         scratch_shapes=[
-            pltpu.VMEM((2 * half, 4, 128), f32),
+            pltpu.VMEM((2 * half * 4, 128), f32),
             pltpu.VMEM((4 * half, snps), bf16),
             pltpu.VMEM((9 * genes, half), bf16),
             pltpu.VMEM((snps, half), bf16),
@@ -370,8 +495,8 @@
             pltpu.VMEM((snps, 128), f32),
             pltpu.VMEM((snps, 128), f32),
             pltpu.VMEM((8, snps), f32),
-            pltpu.VMEM((STEP, 4, 128), f32),
-            pltpu.VMEM((STEP, 4, 128), f32),
+            pltpu.VMEM((4 * STEP, 128), f32),
+            pltpu.VMEM((4 * STEP, 128), f32),
             pltpu.VMEM((2 * labels, 256, 256), f32),
             pltpu.VMEM((2 * labels, 256, 256), f32),
             pltpu.VMEM((labels, 256, 256), f32),
@@ -381,13 +506,16 @@
             pltpu.VMEM((18, 8, 128), f32),
             pltpu.VMEM((8, 128), f32),
             pltpu.VMEM((8, 128), f32),
-            dma((8,)), dma((8,)), dma((4,)), dma((4,)), dma((3,)), dma((3,)),
+            dma((20,)), dma((18,)), dma((4,)), dma((4,)), dma((3,)), dma((3,)),
             dma((10,)), dma((10,)), dma((16,)), dma((18,)), dma(()),
         ],
         compiler_params=pltpu.CompilerParams(
             collective_id=0, has_side_effects=True, vmem_limit_bytes=64 * 1024 * 1024 - 65536
         ),
-    )(inverse.reshape(-1), phenotypes, genotypes, environment.reshape(-1, 128), mask)
+    )(
+        inverse.reshape(-1), chrom_bounds, phenotypes, genotypes, environment.reshape(-1, 128),
+        window_start.reshape(-1, 128), window_end.reshape(-1, 128),
+    )
 
 
 def solution(mesh):

time: 133 us -> 73.9 us (0.56)
  Pallas kernels: 126 us -> 70 us
  other arithmetic: 3.21 us -> 0 us
    pallas_call x1, Pallas kernels: 121 us -> 65.5 us  [shards(): pl.pallas_call(scan_kernel, name='scan', out_shape=jax.ShapeDtypeStruct((...]
  transfers between devices with their start and end apart: 1 -> 1, of which waited for: 0 -> 1; matrix products, arithmetic and copies ran while one was open for 3% -> 0% of each run, Pallas kernels for 0% -> 0%
where the time goes in v2:
time: 73.9 us; the launch traced here: 73.7 us
  Pallas kernels  70 us (95%)
  local copies, waits for them, and re-layouts  1.89 us (3%)
  waiting for transfers between devices  1.11 us (2%)
    pallas_call x1, Pallas kernels, shards(): pl.pallas_call(scan_kernel, name='scan', out_shape=jax.ShapeDtypeStruct((...  65.5 us
    pallas_call x1, Pallas kernels, shards(): pl.pallas_call(inverse_kernel, name='invert', out_shape=jax.ShapeDtypeStr...  4.53 us
    unnamed x3, local copies, waits for them, and re-layouts  1.89 us
  transfers between devices with their start and end apart: 1, of which 1 were waited for; matrix products, arithmetic and copies ran while one was open for 0% of the time, Pallas kernels for 0%

profile of v2, /device:TPU:97, one launch (start us, length us, event | category | flops | bytes accessed | tf_op | source)
XLA Modules:
  0.0 73.7 jit_solution(4894335053819444461)
XLA Ops:
  0.0 0.7 collective-permute-start
  0.7 1.1 %collective-permute-done.other_ref = s32[4,4096]{1,0:T(4,128)S(1)} collective-permute-done((s32[4,4096]{1,0:T(4,128)}, s32[4,4096]{1,0:T(4,128)S(1)}, u32[]{:S(2)}, u32[]{:S(2)}) %collective-permute-start) | collective-permute-done | bytes 65568 | tf_op jit(solution)/shard_map/ppermute | solution.py:471
  1.8 0.0 copy-start
  1.8 0.6 copy-done
  2.4 4.5 %invert.1 = s32[128,128]{1,0:T(8,128)} custom-call(s32[4,4096]{1,0:T(4,128)} %own_ref.1, s32[4,4096]{1,0:T(4,128)} %copy-done), custom_call_target="tpu_custom_call" | custom-call | tf_op jit(solution)/shard_map/invert/pallas_call | solution.py:472
  6.9 65.5 %scan.1 = f32[5,64]{1,0:T(8,128)} custom-call(s32[16384]{0:T(1024)} %bitcast.4, s32[21]{0:T(128)} %bounds_ref.1, bf16[64,4096]{1,0:T(8,128)(2,1)} %y_ref.1, bf16[512,4096]{1,0:T(8,128)(2,1)} %g_ref.1, f32[32,128]{1,0:T(8,128)} %bitcast.5, s32[32,128]{1,0:T(8,128)} %bitcast.6, s32[32,128]{1,0:T(8,128)} %bitcast.7), custom_call_target="tpu_custom_call" | custom-call | tf_op jit(solution)/shard_map/scan/pallas_call | solution.py:482
  72.5 1.3 %copy.9 = f32[5,64]{1,0:T(8,128)} copy(f32[5,64]{1,0:T(8,128)} %scan.1) | data formatting | bytes 2560
Async XLA Ops:
  0.0 1.8 %collective-permute-start = (s32[4,4096]{1,0:T(4,128)}, s32[4,4096]{1,0:T(4,128)S(1)}, u32[]{:S(2)}, u32[]{:S(2)}) collective-permute-start(s32[4,4096]{1,0:T(4,128)} %own_ref.1), channel_id=1, source_target_pairs={{0,1},{1,0},{2,3},{3,2},{4,5},{5,4},{6,7},{7,6},{8,9},{9,8},{10,11... | collective-permute-start | bytes 196616 | tf_op jit(solution)/shard_map/ppermute | solution.py:471
  1.8 0.6 copy-start

commit v3 on v1

v3 whole, which is shorter than its diff:
```python
import functools

import jax
import jax.numpy as jnp
from jax import lax
from jax.experimental import pallas as pl
from jax.experimental.pallas import tpu as pltpu
from jax.sharding import PartitionSpec as P

SNP_BLOCK = 256
MESH = pl.DeviceIdType.MESH
SLOTS = (
    (-4, 3, 0, 1, 4, 2, -3, -2, -1),
    (-4, -1, 0, 1, 4, 2, -3, 3, -2),
    (-4, -1, 0, 1, 4, -2, -3, 3, 2),
    (-4, -1, 0, -3, 4, -2, 3, 2, 1),
)
CORE_SLOTS = ((0, 1, 2, 3, 5, 6, 7, 8), (1, 2, 3, 4, 5, 6, 7, 8))
STEP = 512
FAR_STEP = 1024


def when(condition, action):
    if condition is None:
        action()
    else:
        pl.when(condition)(action)


def remote(src, dst, send, recv, target):
    return pltpu.make_async_remote_copy(
        src, dst, send, recv, device_id=target, device_id_type=MESH
    )


def row_places(me, indices):
    place = lax.rem(me, 4)
    line = lax.div(me, 4)
    left = me - place + lax.rem(place + 3, 4)
    right = me - place + lax.rem(place + 1, 4)
    return place, left, right, line > 0, line < indices // 4 - 1


def residuals(source, weights, reg_ref, h_ref, k, first):
    for s in range(2):
        start = pl.multiple_of(k * 256 + s * 128, 128)
        weight = weights[pl.ds(k * 2 + s, 1), :]
        for q in range(4):
            rows = slice(q * 128, (q + 1) * 128)
            value = source[rows, pl.ds(start, 128)].astype(jnp.float32)
            value = jnp.transpose(value * (weight - reg_ref[rows, :]))
            h_ref[pl.ds((first + start) * 4 + q, 128, stride=4), :] = value


def exchange_kernel(
    shuffles_ref, env_ref, y_hbm, g_hbm,
    inv_ref, near_hbm, other_hbm, own_hbm, env_out, reg_ref, div_ref, pow_out,
    shuffles_other, env_other, y_ref, g_ref, h_ref, mom_ref, mom_other, pow_ref, pow_other,
    local_sem, h_sem, y_send, y_recv, g_send, g_recv, s_send, s_recv,
):
    me = lax.axis_index("genome")
    core = lax.axis_index("sample")
    indices = lax.axis_size("genome")
    sib = (me, 1 - core)
    perms, half = shuffles_ref.shape
    snps = g_hbm.shape[0]
    genes = y_hbm.shape[0]
    place, left, right, above, below = row_places(me, indices)
    part = snps // 4
    g_loads = [
        pltpu.make_async_copy(
            g_hbm.at[pl.ds(i * part, part), :], g_ref.at[pl.ds(i * part, part), :], local_sem.at[i]
        )
        for i in range(4)
    ]
    y_load = pltpu.make_async_copy(y_hbm, y_ref, local_sem.at[4])
    y_load.start()
    for copy in g_loads:
        copy.start()

    barrier = pltpu.get_barrier_semaphore()
    for target in (sib, (left, core), (right, core)):
        pl.semaphore_signal(barrier, inc=1, device_id=target, device_id_type=MESH)
    pl.when(above)(
        lambda: pl.semaphore_signal(barrier, inc=1, device_id=(me - 4, core), device_id_type=MESH)
    )
    pl.when(below)(
        lambda: pl.semaphore_signal(barrier, inc=1, device_id=(me + 4, core), device_id_type=MESH)
    )
    pl.semaphore_wait(barrier, 3 + jnp.where(above, 1, 0) + jnp.where(below, 1, 0))

    shuffle_copy = remote(shuffles_ref, shuffles_other, s_send.at[0], s_recv.at[0], sib)
    env_copy = remote(env_ref, env_other, s_send.at[1], s_recv.at[1], sib)
    shuffle_copy.start()
    env_copy.start()
    piece = genes // 2
    y_copies = []
    for h in range(2):
        for slot, target, sent, got in (
            (1, right, None, None), (2, left, None, None), (0, me + 4, below, above), (3, me - 4, above, below),
        ):
            copy = remote(
                y_hbm.at[pl.ds(h * piece, piece), :], near_hbm.at[pl.ds(slot * genes + h * piece, piece), :],
                y_send.at[2 * slot + h], y_recv.at[2 * slot + h], (target, core),
            )
            when(sent, copy.start)
            y_copies.append((sent, got, copy))
    g_copies = [
        remote(
            g_hbm.at[pl.ds(i * part, part), :], other_hbm.at[pl.ds(i * part, part), :],
            g_send.at[i], g_recv.at[i], sib,
        )
        for i in range(4)
    ]
    for copy in g_copies:
        copy.start()

    lane = lax.broadcasted_iota(jnp.int32, (64, 128), 1)

    def moments(block, _):
        first = pl.multiple_of(block * 64, 64)
        square = jnp.zeros((64, 128), jnp.float32)
        cross = square
        inter = square
        for column in range(half // 128):
            value = g_ref[pl.ds(first, 64), column * 128 : (column + 1) * 128].astype(jnp.float32)
            weight = env_ref[column : column + 1, :]
            value = value * value
            once = value * weight
            square += value
            cross += once
            inter += once * weight
        square = jnp.sum(square, axis=1, keepdims=True)
        cross = jnp.sum(cross, axis=1, keepdims=True)
        inter = jnp.sum(inter, axis=1, keepdims=True)
        mom_ref[pl.ds(first, 64), :] = jnp.where(lane == 0, square, jnp.where(lane == 1, cross, inter))
        return 0

    for copy in g_loads:
        copy.wait()
    lax.fori_loop(0, snps // 64, moments, 0)
    mom_copy = remote(mom_ref, mom_other, s_send.at[2], s_recv.at[2], sib)
    mom_copy.start()

    y_load.wait()
    power = jnp.zeros((genes, 128), jnp.float32)
    for column in range(half // 128):
        value = y_ref[:, column * 128 : (column + 1) * 128].astype(jnp.float32)
        power += value * value
    power = jnp.broadcast_to(jnp.sum(power, axis=1, keepdims=True), (genes, 128))
    power = jnp.concatenate([power, power], axis=0)
    pow_ref[...] = jnp.transpose(power)[0:8, :]
    pow_copy = remote(pow_ref, pow_other, s_send.at[3], s_recv.at[3], sib)
    pow_copy.start()

    width = 2048
    rows = half // 128

    def located(ref, p, offset):
        total = jnp.zeros((2 * rows, 128), jnp.float32)
        for start in range(0, half, width):
            target = ref[p : p + 1, start : start + width]
            high = (target >> 7) - rows * core
            low = target & 127
            spot = lax.broadcasted_iota(jnp.int32, (1, width), 1) + (offset + start)
            hit = lax.broadcasted_iota(jnp.int32, (rows, width), 0) == high
            spot_high = (spot >> 7).astype(jnp.float32)
            spot_low = (spot & 127).astype(jnp.float32)
            lhs = jnp.concatenate(
                [jnp.where(hit, spot_high, 0.0), jnp.where(hit, spot_low, 0.0)], axis=0
            ).astype(jnp.bfloat16)
            rhs = jnp.where(
                lax.broadcasted_iota(jnp.int32, (128, width), 0) == low, 1.0, 0.0
            ).astype(jnp.bfloat16)
            total += lax.dot_general(
                lhs, rhs, (((1,), (1,)), ((), ())), preferred_element_type=jnp.float32
            )
        return total

    totals = [located(shuffles_ref, p, 0) for p in range(perms)]
    mom_copy.wait_recv()
    for q in range(4):
        lines = slice(q * 128, (q + 1) * 128)
        total = mom_ref[lines, :] + mom_other[lines, :]
        square, cross, inter = total[:, 0:1], total[:, 1:2], total[:, 2:3]
        regression = cross / square
        divisor = inter - cross * regression + 0.1 * inter
        reg_ref[lines, :] = jnp.broadcast_to(regression, (128, 128))
        div_ref[:, lines] = jnp.transpose(jnp.broadcast_to(divisor, (128, 128)))[0:8, :]

    def own_residuals(k, _):
        residuals(g_ref, env_ref, reg_ref, h_ref, k, 0)
        return 0

    h_copies = []
    for i in range(4):
        lax.fori_loop(i * half // 1024, (i + 1) * half // 1024, own_residuals, 0)
        copy = pltpu.make_async_copy(
            h_ref.at[pl.ds(i * half, half), :], own_hbm.at[pl.ds(i * half, half), :], h_sem.at[i]
        )
        copy.start()
        h_copies.append(copy)

    shuffle_copy.wait_recv()
    for p in range(perms):
        total = totals[p] + located(shuffles_other, p, half)
        inv_ref[p * rows : (p + 1) * rows, :] = (
            total[:rows] * 128.0 + total[rows:]
        ).astype(jnp.int32) * 4

    env_copy.wait_recv()
    env_out[...] = env_other[...]
    pow_copy.wait_recv()
    pow_out[...] = pow_ref[...] + pow_other[...]
    for copy in h_copies:
        copy.wait()
    for copy in g_copies:
        copy.wait_recv()
    for sent, got, copy in y_copies:
        when(got, copy.wait_recv)
    for copy in g_copies + [shuffle_copy, env_copy, mom_copy, pow_copy]:
        copy.wait_send()
    for sent, got, copy in y_copies:
        when(sent, copy.wait_send)


def scan_kernel(
    inv_hbm, bounds_ref, y_hbm, other_hbm, own_hbm, near_hbm, env_other, reg_ref, div_ref, pow_ref, start_ref, end_ref,
    out_ref,
    index0, index1, h_ref, gp_ref, band_ref, other_ref,
    stage0, stage1, near_acc, far_acc, near_in, far_in, peak_ref, msg_ref, msg_in,
    y_send, y_recv, p_send, p_recv, m_send, m_recv, band_sem, g_sem, index_sem,
):
    me = lax.axis_index("genome")
    core = lax.axis_index("sample")
    indices = lax.axis_size("genome")
    sib = (me, 1 - core)
    genes, half = y_hbm.shape
    snps = other_hbm.shape[0]

    def inside(o):
        return (me + o >= 0) & (me + o < indices)

    barrier = pltpu.get_barrier_semaphore()
    pl.semaphore_signal(barrier, inc=1, device_id=sib, device_id_type=MESH)
    count = jnp.int32(1)
    for o in range(-4, 5):
        if o != 0:
            for k in range(2):
                @pl.when(inside(o))
                def _(o=o, k=k):
                    pl.semaphore_signal(barrier, inc=1, device_id=(me + o, k), device_id_type=MESH)
            count = count + jnp.where(inside(o), 2, 0)

    place, _, _, above, below = row_places(me, indices)
    piece = genes // 2
    hops = []

    def arrival(slot, part):
        return remote(
            y_hbm.at[pl.ds(0, piece), :], band_ref.at[pl.ds(slot * genes + part * piece, piece), :],
            y_send.at[0], y_recv.at[2 * (slot - 5) + part], sib,
        )

    def hop(x, link, shift, part):
        step = {"right": 1, "left": -1, "up": -4, "down": 4}[link]
        needs = set()
        if link in ("right", "left"):
            other = (x + step) % 4
            step = other - x
        else:
            other = x
            needs.add(link)
        if not 0 <= x + shift < 4:
            needs.add("up" if x + shift < 0 else "down")
        here = SLOTS[x].index(shift)
        there = SLOTS[other].index(shift - step)
        index = sum(1 for at, _ in hops if at == x)
        if here in (0, 1, 3, 4):
            source = near_hbm.at[pl.ds((0, 1, 0, 2, 3)[here] * genes + part * piece, piece), :]
        else:
            source = band_ref.at[pl.ds(here * genes + part * piece, piece), :]
        copy = remote(
            source, band_ref.at[pl.ds(there * genes + part * piece, piece), :],
            y_send.at[index], y_recv.at[2 * (there - 5) + part], (me + step, core),
        )
        when(rows_exist(needs), copy.start)
        hops.append((x, needs))

    def rows_exist(needs):
        if needs == {"up", "down"}:
            return above & below
        return {"up": above, "down": below}[min(needs)] if needs else None

    def finish_hops():
        for x in range(4):
            @pl.when(place == x)
            def _(x=x):
                for index, needs in enumerate([needs for at, needs in hops if at == x]):
                    copy = remote(
                        y_hbm.at[pl.ds(0, piece), :], band_ref.at[pl.ds(0, piece), :],
                        y_send.at[index], y_recv.at[0], sib,
                    )
                    when(rows_exist(needs), copy.wait_send)

    def second_hops():
        for x in range(4):
            @pl.when(place == x)
            def _(x=x):
                left, right = SLOTS[x][1], SLOTS[x][3]
                hop(x, "right", left, 1)
                hop(x, "left", right, 0)
                if x < 3:
                    for part in ((0, 1) if x == 0 else (1, 0)):
                        hop(x, "down", right, part)
                if x > 0:
                    for part in ((1, 0) if x == 3 else (0, 1)):
                        hop(x, "up", left, part)
                if x == 3:
                    hop(x, "right", -4, 0)
                    hop(x, "right", -4, 1)
                if x == 0:
                    hop(x, "left", 4, 0)
                    hop(x, "left", 4, 1)

    def third_hops():
        for part in range(2):
            arrival(5, part).wait_recv()
        for x in range(4):
            @pl.when(place == x)
            def _(x=x):
                if x == 0:
                    hop(x, "down", 2, 0)
                if x == 1:
                    hop(x, "down", 2, 0)
                if x == 2:
                    hop(x, "up", -2, 1)
                if x == 3:
                    hop(x, "up", -2, 1)
        middle = (place == 1) | (place == 2)
        for slot, part, exists in ((6, 1, above), (7, 0, below)):
            pl.when(middle & exists)(arrival(slot, part).wait_recv)
        for x in (1, 2):
            @pl.when(place == x)
            def _(x=x):
                hop(x, "left", -3, 1)
                hop(x, "right", 3, 0)

    def last_arrivals():
        for slot in (6, 7, 8):
            for part in range(2):
                early = {(6, 1): True, (7, 0): True}.get((slot, part), False)
                copy = arrival(slot, part)
                for x in range(4):
                    if early and x in (1, 2):
                        continue
                    o = SLOTS[x][slot]
                    exists = above if x + o < 0 else below
                    pl.when((place == x) & exists)(copy.wait_recv)

    band_loads = [pltpu.make_async_copy(y_hbm, band_ref.at[pl.ds(2 * genes, genes), :], band_sem.at[0])]
    for i, slot in enumerate((0, 1, 3, 4)):
        band_loads.append(pltpu.make_async_copy(
            near_hbm.at[pl.ds(i * genes, genes), :], band_ref.at[pl.ds(slot * genes, genes), :],
            band_sem.at[1 + i],
        ))
    width = half // 8
    other_loads = [
        pltpu.make_async_copy(
            other_hbm.at[:, pl.ds(i * width, width)], other_ref.at[:, pl.ds(i * width, width)], g_sem.at[i]
        )
        for i in range(8)
    ]
    own_load = pltpu.make_async_copy(own_hbm, h_ref.at[pl.ds(0, 4 * half), :], band_sem.at[5])
    index_rows = 1024
    blocks = 4 * half // index_rows

    def index_load(ref, slot, k):
        return pltpu.make_async_copy(
            inv_hbm.at[pl.ds(pl.multiple_of(k * index_rows, index_rows), index_rows)], ref, index_sem.at[slot]
        )

    for copy in other_loads:
        copy.start()
    own_load.start()
    for copy in band_loads:
        copy.start()
    index_load(index0, 0, 0).start()
    index_load(index1, 1, 1).start()

    def other_residuals(k, _):
        residuals(other_ref, env_other, reg_ref, h_ref, k, half)
        return 0

    near_acc[...] = jnp.zeros_like(near_acc)
    far_acc[...] = jnp.zeros_like(far_acc)
    for i, copy in enumerate(other_loads):
        copy.wait()
        lax.fori_loop(i * width // 256, (i + 1) * width // 256, other_residuals, 0)
        if i == 1:
            pl.semaphore_wait(barrier, count)
            second_hops()
    own_load.wait()
    for copy in band_loads:
        copy.wait()

    def right_side(ref, first, b, count):
        return jnp.concatenate(
            [ref[pl.ds(first + 2 * b + i, count, stride=4), :] for i in range(2)], axis=1
        ).astype(jnp.bfloat16)

    def gather(stage, index, offset):
        for t in range(STEP):
            stage[4 * t : 4 * t + 4, :] = h_ref[pl.ds(index[offset + t], 4), :]

    def settle(stage, n):
        for q in range(4):
            gp_ref[pl.ds(pl.multiple_of((n + 1) * STEP, STEP), STEP), 128 * q : 128 * q + 128] = (
                stage[pl.ds(q, STEP, stride=4), :].astype(jnp.bfloat16)
            )

    def product(acc, rows, label, k, base, plain):
        start = pl.multiple_of(k * FAR_STEP, FAR_STEP)
        for b in range(2):
            lhs = band_ref[rows[b] : rows[b] + 256, pl.ds(start, FAR_STEP)]
            if plain:
                rhs = right_side(h_ref, start * 4, b, FAR_STEP)
            else:
                rhs = gp_ref[pl.ds(pl.multiple_of(base + start, STEP), FAR_STEP), 256 * b : 256 * b + 256]
            acc[2 * label + b] += jnp.dot(lhs, rhs, preferred_element_type=jnp.float32)

    near_rows, far_rows = (0, 64), (320, 320)

    def permuted(i, _, plain=False):
        for s, (index, slot) in enumerate(((index0, 0), (index1, 1))):
            index_load(index, slot, 2 * i + s).wait()
            n = 4 * i + 2 * s
            gather(stage0, index, 0)
            settle(stage1, n - 1)
            label = lax.div(i, 2)
            product(near_acc, near_rows, label, lax.rem(2 * i + s, 4), STEP + (label - 1) * half, plain)
            gather(stage1, index, STEP)
            settle(stage0, n)
            index_load(index, slot, lax.rem(2 * i + s + 2, blocks)).start()
        return 0

    lax.fori_loop(0, 2, functools.partial(permuted, plain=True), 0)
    third_hops()
    lax.fori_loop(2, blocks // 2, permuted, 0)
    settle(stage1, 4 * half // STEP - 1)
    index_load(index0, 0, 0).wait()
    index_load(index1, 1, 1).wait()

    def last_near(k, _):
        product(near_acc, near_rows, 4, k, STEP + 3 * half, False)
        return 0

    lax.fori_loop(0, half // FAR_STEP, last_near, 0)

    partials = []
    for label in range(5):
        copy = remote(
            near_acc.at[2 * label + 1 - core], near_in.at[label], p_send.at[label], p_recv.at[label], sib
        )
        copy.start()
        partials.append(copy)
    last_arrivals()

    for label in range(5):
        def distant(k, _, label=label):
            product(far_acc, far_rows, label, k, STEP + (label - 1) * half, label == 0)
            return 0

        lax.fori_loop(0, half // FAR_STEP, distant, 0)
        copy = remote(
            far_acc.at[2 * label + 1 - core], far_in.at[label], p_send.at[5 + label], p_recv.at[5 + label], sib
        )
        copy.start()
        partials.append(copy)

    divisor = div_ref[0:1, pl.ds(pl.multiple_of(core * 256, 256), 256)]
    lanes = lax.broadcasted_iota(jnp.int32, (256, 128), 1)
    for part, (acc, arrived) in enumerate(((near_acc, near_in), (far_acc, far_in))):
        peaks = jnp.zeros((256, 128), jnp.float32)
        for label in range(5):
            partials[5 * part + label].wait_recv()
            numerator = acc[2 * label + core] + arrived[label]
            scores = numerator * numerator / divisor
            peaks = jnp.where(lanes == label, jnp.max(scores, axis=1, keepdims=True), peaks)
        peak_ref[:, 256 * part : 256 * part + 128] = jnp.transpose(peaks[0:128])[0:8, :]
        peak_ref[:, 256 * part + 128 : 256 * part + 256] = jnp.transpose(peaks[128:256])[0:8, :]
    msg_ref[...] = jnp.zeros_like(msg_ref)
    shifts = [sum(jnp.where(place == x, SLOTS[x][slot], 0) for x in range(4)) for slot in range(9)]
    block = me * (snps // SNP_BLOCK) + core
    total_blocks = indices * (snps // SNP_BLOCK)
    for s in range(8):
        shift = jnp.where(core == 0, shifts[CORE_SLOTS[0][s]], shifts[CORE_SLOTS[1][s]])
        owner = jnp.clip(me + shift, 0, indices - 1)
        odd = lax.rem(owner, 2) == 1
        begin = start_ref[pl.ds(lax.div(owner, 2), 1), :]
        finish = end_ref[pl.ds(lax.div(owner, 2), 1), :]
        begin = jnp.where(odd, begin[:, 64:128], begin[:, 0:64])
        finish = jnp.where(odd, finish[:, 64:128], finish[:, 0:64])
        middle = (begin + finish - 1) >> 1
        lower = jnp.zeros_like(middle)
        upper = jnp.full_like(middle, total_blocks)
        for k in range(bounds_ref.shape[0]):
            bound = bounds_ref[k]
            before = bound <= middle
            lower = jnp.maximum(lower, jnp.where(before, bound, 0))
            upper = jnp.minimum(upper, jnp.where(before, total_blocks, bound))
        inner = (jnp.maximum(begin, lower) <= block) & (block < jnp.minimum(finish, upper))
        msg_ref[s, :, 0:64] = jnp.where(inner, peak_ref[:, 64 * s : 64 * s + 64], 0.0)

    sends = []
    for c in range(2):
        for s in range(8):
            for k in range(2):
                local = CORE_SLOTS[c][s] == 2
                if local and k == c:
                    continue
                shift = shifts[CORE_SLOTS[c][s]]
                copy = remote(
                    msg_ref.at[s], msg_in.at[2 * (shift + 4) + c], m_send.at[2 * s + k],
                    m_recv.at[2 * (shift + 4) + c], (me + shift, k),
                )
                condition = (core == c) & inside(shift)
                when(condition, copy.start)
                sends.append((condition, copy))

    best = jnp.where(core == 0, msg_ref[2], msg_ref[1])
    for c in range(2):
        for o in range(-4 + c, 4 + c):
            index = 2 * (o + 4) + c
            condition = (core == 1 - c) if o == 0 else inside(-o)
            copy = remote(msg_ref.at[0], msg_in.at[index], m_send.at[0], m_recv.at[index], sib)
            when(condition, copy.wait_recv)
            best = jnp.maximum(best, jnp.where(condition, msg_in[index], 0.0))
    result = jnp.sqrt(best / (pow_ref[...] / (2.0 * half) + 1e-05))
    out_ref[...] = result[0:5, 0:64]

    for copy in partials:
        copy.wait_send()
    finish_hops()
    for condition, copy in sends:
        when(condition, copy.wait_send)


def shards(genotypes, phenotypes, environment, shuffles, window_start, window_end, chrom_bounds):
    snps, half = genotypes.shape
    genes = phenotypes.shape[0]
    labels = shuffles.shape[0] + 1
    vmem = pl.BlockSpec(memory_space=pltpu.VMEM)

    f32, bf16, i32 = jnp.float32, jnp.bfloat16, jnp.int32
    dma = pltpu.SemaphoreType.DMA
    shape = jax.ShapeDtypeStruct
    anywhere = pl.BlockSpec(memory_space=pl.ANY)
    smem = pl.BlockSpec(memory_space=pltpu.SMEM)
    weights = environment.reshape(-1, 128)
    lines = half // 128
    inverse, near, other, own, weights_other, slopes, divisors, power = pl.pallas_call(
        exchange_kernel,
        name="exchange",
        out_shape=(
            shape(((labels - 1) * lines, 128), i32),
            shape((4 * genes, half), bf16),
            shape((snps, half), bf16),
            shape((4 * half, 128), f32),
            shape((lines, 128), f32),
            shape((snps, 128), f32),
            shape((8, snps), f32),
            shape((8, 128), f32),
        ),
        in_specs=[vmem, vmem, anywhere, anywhere],
        out_specs=(vmem, anywhere, anywhere, anywhere, vmem, vmem, vmem, vmem),
        scratch_shapes=[
            pltpu.VMEM((labels - 1, half), i32),
            pltpu.VMEM((lines, 128), f32),
            pltpu.VMEM((genes, half), bf16),
            pltpu.VMEM((snps, half), bf16),
            pltpu.VMEM((4 * half, 128), f32),
            pltpu.VMEM((snps, 128), f32),
            pltpu.VMEM((snps, 128), f32),
            pltpu.VMEM((8, 128), f32),
            pltpu.VMEM((8, 128), f32),
            dma((5,)), dma((4,)), dma((8,)), dma((8,)), dma((4,)), dma((4,)), dma((4,)), dma((4,)),
        ],
        compiler_params=pltpu.CompilerParams(
            collective_id=1, has_side_effects=True, vmem_limit_bytes=64 * 1024 * 1024 - 65536
        ),
    )(shuffles, weights, phenotypes, genotypes)

    return pl.pallas_call(
        scan_kernel,
        name="scan",
        out_shape=shape((labels, genes), f32),
        in_specs=[anywhere, smem] + [anywhere] * 4 + [vmem] * 6,
        out_specs=vmem,
        scratch_shapes=[
            pltpu.SMEM((1024,), i32),
            pltpu.SMEM((1024,), i32),
            pltpu.VMEM((2 * half * 4, 128), f32),
            pltpu.VMEM((4 * half + STEP, snps), bf16),
            pltpu.VMEM((9 * genes, half), bf16),
            pltpu.VMEM((snps, half), bf16),
            pltpu.VMEM((4 * STEP, 128), f32),
            pltpu.VMEM((4 * STEP, 128), f32),
            pltpu.VMEM((2 * labels, 256, 256), f32),
            pltpu.VMEM((2 * labels, 256, 256), f32),
            pltpu.VMEM((labels, 256, 256), f32),
            pltpu.VMEM((labels, 256, 256), f32),
            pltpu.VMEM((8, 8 * genes), f32),
            pltpu.VMEM((8, 8, 128), f32),
            pltpu.VMEM((18, 8, 128), f32),
            dma((16,)), dma((8,)), dma((10,)), dma((10,)), dma((16,)), dma((18,)),
            dma((6,)), dma((8,)), dma((2,)),
        ],
        compiler_params=pltpu.CompilerParams(
            collective_id=0, has_side_effects=True, vmem_limit_bytes=64 * 1024 * 1024 - 65536
        ),
    )(
        inverse.reshape(-1), chrom_bounds, phenotypes, other, own, near, weights_other, slopes, divisors,
        power, window_start.reshape(-1, 128), window_end.reshape(-1, 128),
    )


def solution(mesh):
    placed = (
        P("genome", "sample"),
        P("genome", "sample"),
        P("sample"),
        P(None, "sample"),
        P(),
        P(),
        P(),
    )
    return jax.shard_map(
        shards, mesh=mesh, in_specs=placed, out_specs=P(None, "genome"), check_vma=False
    )
```

time: 133 us -> 66.4 us (0.50)
  Pallas kernels: 126 us -> 64.8 us
  other arithmetic: 3.21 us -> 0 us
  local copies, waits for them, and re-layouts: 2.75 us -> 1.27 us
    pallas_call x2, Pallas kernels: 126 us -> 64.8 us  [the longest x1 46.1 us: shards(): pl.pallas_call(scan_kernel, name='scan', out_shape=shape((labels, genes),...]
  transfers between devices with their start and end apart: 1 -> 0, of which waited for: 0 -> 0; matrix products, arithmetic and copies ran while one was open for 3% -> 0% of each run, Pallas kernels for 0% -> 0%
where the time goes in v3:
time: 66.4 us; the launch traced here: 66.1 us
  Pallas kernels  64.8 us (98%)
  local copies, waits for them, and re-layouts  1.27 us (2%)
    pallas_call x1, Pallas kernels, shards(): pl.pallas_call(scan_kernel, name='scan', out_shape=shape((labels, genes),...  46.1 us
    pallas_call x1, Pallas kernels, shards(): pl.pallas_call(exchange_kernel, name='exchange', out_shape=(shape(((label...  18.8 us

profile of v3, /device:TPU:97, one launch (start us, length us, event | category | flops | bytes accessed | tf_op | source)
XLA Modules:
  0.0 66.1 jit_solution(8453534533200029193)
XLA Ops:
  0.0 18.8 %exchange.1 = (s32[128,128]{1,0:T(8,128)}, bf16[256,4096]{1,0:T(8,128)(2,1)}, bf16[512,4096]{1,0:T(8,128)(2,1)}, f32[16384,128]{1,0:T(8,128)}, f32[32,128]{1,0:T...) custom-call(s32[4,4096]{1,0:T(4,128)} %shuffles_ref.1, f32[32,128]{1,0:T(8,128)} %bitcast.5, ...), custom_call_target="tpu_custom_call" | custom-call | tf_op jit(solution)/shard_map/exchange/pallas_call | solution.py:562
  18.8 46.1 %scan.1 = f32[5,64]{1,0:T(8,128)} custom-call(s32[16384]{0:T(1024)} %bitcast.4, s32[21]{0:T(128)} %bounds_ref.1, bf16[64,4096]{1,0:T(8,128)(2,1)} %y_hbm.3, bf16[512,4096]{1,0:T(8,128)(2,1)} %get-tuple-element.14.other_hbm, f32[16384,128]{1,0:T(8,128)} %get-tuple-element.15.own_hbm, bf16[256,4096]{1,0:T(8,128)(2,1)} %get-tuple-element.16.near_hbm, ...), custom_call_target="tpu_custom_call" | custom-call | tf_op jit(solution)/shard_map/scan/pallas_call | solution.py:594
  64.9 1.3 %copy.9 = f32[5,64]{1,0:T(8,128)} copy(f32[5,64]{1,0:T(8,128)} %scan.1) | data formatting | bytes 2560

commit v4 on v2

v4 whole, which is shorter than its diff:
```python
import functools

import jax
import jax.numpy as jnp
from jax import lax
from jax.experimental import pallas as pl
from jax.experimental.pallas import tpu as pltpu
from jax.sharding import PartitionSpec as P

SNP_BLOCK = 256
MESH = pl.DeviceIdType.MESH
SLOTS = (
    (-4, 3, 0, 1, 4, 2, -3, -2, -1),
    (-4, -1, 0, 1, 4, 2, -3, 3, -2),
    (-4, -1, 0, 1, 4, -2, -3, 3, 2),
    (-4, -1, 0, -3, 4, -2, 3, 2, 1),
)
CORE_SLOTS = ((0, 1, 2, 3, 5, 6, 7, 8), (1, 2, 3, 4, 5, 6, 7, 8))
STEP = 512
FAR_STEP = 1024
SPLIT = 3


def when(condition, action):
    if condition is None:
        action()
    else:
        pl.when(condition)(action)


def remote(src, dst, send, recv, target):
    return pltpu.make_async_remote_copy(
        src, dst, send, recv, device_id=target, device_id_type=MESH
    )


def residuals(source, weights, reg_ref, h_ref, k, first):
    for s in range(2):
        start = pl.multiple_of(k * 256 + s * 128, 128)
        weight = weights[pl.ds(k * 2 + s, 1), :]
        for q in range(4):
            rows = slice(q * 128, (q + 1) * 128)
            value = source[rows, pl.ds(start, 128)].astype(jnp.float32)
            value = jnp.transpose(value * (weight - reg_ref[rows, :]))
            h_ref[pl.ds((first + start) * 4 + q, 128, stride=4), :] = value


def scan_kernel(
    bounds_ref, shuffles_ref, env_ref, start_ref, end_ref, y_hbm, g_hbm,
    out_ref,
    index0, index1, h_ref, gp_ref, band_ref, g_ref, other_ref, shuffles_other, env_other, inv_ref,
    mom_ref, mom_other, reg_ref, div_ref, pow_ref, pow_other,
    stage0, stage1, near_acc, far_acc, near_in, far_in, peak_ref, msg_ref, msg_in,
    y_send, y_recv, g_send, g_recv, s_send, s_recv, p_send, p_recv, m_send, m_recv,
    local_sem, index_sem,
):
    me = lax.axis_index("genome")
    core = lax.axis_index("sample")
    indices = lax.axis_size("genome")
    sib = (me, 1 - core)
    perms, half = shuffles_ref.shape
    genes = y_hbm.shape[0]
    snps = g_hbm.shape[0]
    quarter = snps // 4
    g_loads = [
        pltpu.make_async_copy(
            g_hbm.at[pl.ds(i * quarter, quarter), :], g_ref.at[pl.ds(i * quarter, quarter), :], local_sem.at[i]
        )
        for i in range(4)
    ]
    y_load = pltpu.make_async_copy(y_hbm, band_ref.at[pl.ds(2 * genes, genes), :], local_sem.at[4])
    for copy in g_loads:
        copy.start()
    y_load.start()

    def inside(o):
        return (me + o >= 0) & (me + o < indices)

    barrier = pltpu.get_barrier_semaphore()
    pl.semaphore_signal(barrier, inc=1, device_id=sib, device_id_type=MESH)
    count = jnp.int32(1)
    for o in range(-4, 5):
        if o != 0:
            for k in range(2):
                @pl.when(inside(o))
                def _(o=o, k=k):
                    pl.semaphore_signal(barrier, inc=1, device_id=(me + o, k), device_id_type=MESH)
            count = count + jnp.where(inside(o), 2, 0)
    pl.semaphore_wait(barrier, count)

    place = lax.rem(me, 4)
    line = lax.div(me, 4)
    above, below = line > 0, line < indices // 4 - 1
    piece = genes // 2
    hops = []

    def arrival(slot, part):
        return remote(
            y_hbm.at[pl.ds(0, piece), :], band_ref.at[pl.ds(slot * genes + part * piece, piece), :],
            y_send.at[0], y_recv.at[2 * slot + part], sib,
        )

    def hop(x, link, shift, part):
        step = {"right": 1, "left": -1, "up": -4, "down": 4}[link]
        needs = set()
        if link in ("right", "left"):
            other = (x + step) % 4
            step = other - x
        else:
            other = x
            needs.add(link)
        if not 0 <= x + shift < 4:
            needs.add("up" if x + shift < 0 else "down")
        here = SLOTS[x].index(shift)
        there = SLOTS[other].index(shift - step)
        index = sum(1 for at, _ in hops if at == x)
        if shift == 0:
            source = y_hbm.at[pl.ds(part * piece, piece), :]
        else:
            source = band_ref.at[pl.ds(here * genes + part * piece, piece), :]
        copy = remote(
            source, band_ref.at[pl.ds(there * genes + part * piece, piece), :],
            y_send.at[index], y_recv.at[2 * there + part], (me + step, core),
        )
        when(rows_exist(needs), copy.start)
        hops.append((x, needs))

    def rows_exist(needs):
        if needs == {"up", "down"}:
            return above & below
        return {"up": above, "down": below}[min(needs)] if needs else None

    def finish_hops():
        for x in range(4):
            @pl.when(place == x)
            def _(x=x):
                for index, needs in enumerate([needs for at, needs in hops if at == x]):
                    copy = remote(
                        y_hbm.at[pl.ds(0, piece), :], band_ref.at[pl.ds(0, piece), :],
                        y_send.at[index], y_recv.at[0], sib,
                    )
                    when(rows_exist(needs), copy.wait_send)

    def at_place(x):
        return pl.when(place == x)

    def first_hops():
        for x in range(4):
            @at_place(x)
            def _(x=x):
                for part in range(2):
                    for link in ("right", "left", "down", "up"):
                        hop(x, link, 0, part)

    def second_hops(part):
        arrival(1, part).wait_recv()
        arrival(3, part).wait_recv()
        pl.when(above)(arrival(0, part).wait_recv)
        pl.when(below)(arrival(4, part).wait_recv)
        for x in range(4):
            @at_place(x)
            def _(x=x):
                left, right = SLOTS[x][1], SLOTS[x][3]
                if part == 0:
                    hop(x, "left", right, 0)
                else:
                    hop(x, "right", left, 1)
                if x < 3:
                    hop(x, "down", right, part)
                if x > 0:
                    hop(x, "up", left, part)
                if x == 3:
                    hop(x, "right", -4, part)
                if x == 0:
                    hop(x, "left", 4, part)

    def third_hops():
        for part in range(2):
            arrival(5, part).wait_recv()
        for x in range(4):
            @at_place(x)
            def _(x=x):
                if x < 2:
                    hop(x, "down", 2, 1)
                else:
                    hop(x, "up", -2, 1)
        inner = (place == 1) | (place == 2)
        pl.when(inner & above)(arrival(6, 0).wait_recv)
        pl.when(inner & below)(arrival(7, 0).wait_recv)
        for x in (1, 2):
            @at_place(x)
            def _(x=x):
                hop(x, "left", -3, 0)
                hop(x, "right", 3, 0)

    def last_arrivals():
        for slot in (6, 7, 8):
            for part in range(2):
                early = slot in (6, 7) and part == 0
                copy = arrival(slot, part)
                for x in range(4):
                    if early and x in (1, 2):
                        continue
                    o = SLOTS[x][slot]
                    exists = above if x + o < 0 else below
                    pl.when((place == x) & exists)(copy.wait_recv)

    shuffle_copy = remote(shuffles_ref, shuffles_other, s_send.at[0], s_recv.at[0], sib)
    env_copy = remote(env_ref, env_other, s_send.at[1], s_recv.at[1], sib)
    shuffle_copy.start()
    env_copy.start()
    first_hops()
    g_copies = [
        remote(
            g_hbm.at[pl.ds(i * quarter, quarter), :], other_ref.at[pl.ds(i * quarter, quarter), :],
            g_send.at[i], g_recv.at[i], sib,
        )
        for i in range(4)
    ]
    for copy in g_copies:
        copy.start()

    lane = lax.broadcasted_iota(jnp.int32, (64, 128), 1)

    def moments(block, _):
        first = pl.multiple_of(block * 64, 64)
        square = jnp.zeros((64, 128), jnp.float32)
        cross = square
        inter = square
        for column in range(half // 128):
            value = g_ref[pl.ds(first, 64), column * 128 : (column + 1) * 128].astype(jnp.float32)
            weight = env_ref[column : column + 1, :]
            value = value * value
            once = value * weight
            square += value
            cross += once
            inter += once * weight
        square = jnp.sum(square, axis=1, keepdims=True)
        cross = jnp.sum(cross, axis=1, keepdims=True)
        inter = jnp.sum(inter, axis=1, keepdims=True)
        mom_ref[pl.ds(first, 64), :] = jnp.where(lane == 0, square, jnp.where(lane == 1, cross, inter))
        return 0

    for copy in g_loads:
        copy.wait()
    lax.fori_loop(0, snps // 64, moments, 0)
    mom_copy = remote(mom_ref, mom_other, s_send.at[2], s_recv.at[2], sib)
    mom_copy.start()

    y_load.wait()
    power = jnp.zeros((genes, 128), jnp.float32)
    for column in range(half // 128):
        value = band_ref[2 * genes : 3 * genes, column * 128 : (column + 1) * 128].astype(jnp.float32)
        power += value * value
    power = jnp.broadcast_to(jnp.sum(power, axis=1, keepdims=True), (genes, 128))
    power = jnp.concatenate([power, power], axis=0)
    pow_ref[...] = jnp.transpose(power)[0:8, :]
    pow_copy = remote(pow_ref, pow_other, s_send.at[3], s_recv.at[3], sib)
    pow_copy.start()

    near_acc[...] = jnp.zeros_like(near_acc)
    far_acc[...] = jnp.zeros_like(far_acc)
    width = 2048
    rows = half // 128

    def located(ref, p, offset):
        total = jnp.zeros((2 * rows, 128), jnp.float32)
        for start in range(0, half, width):
            target = ref[p : p + 1, start : start + width]
            high = (target >> 7) - rows * core
            low = target & 127
            spot = lax.broadcasted_iota(jnp.int32, (1, width), 1) + (offset + start)
            hit = lax.broadcasted_iota(jnp.int32, (rows, width), 0) == high
            spot_high = (spot >> 7).astype(jnp.float32)
            spot_low = (spot & 127).astype(jnp.float32)
            lhs = jnp.concatenate(
                [jnp.where(hit, spot_high, 0.0), jnp.where(hit, spot_low, 0.0)], axis=0
            ).astype(jnp.bfloat16)
            rhs = jnp.where(
                lax.broadcasted_iota(jnp.int32, (128, width), 0) == low, 1.0, 0.0
            ).astype(jnp.bfloat16)
            total += lax.dot_general(
                lhs, rhs, (((1,), (1,)), ((), ())), preferred_element_type=jnp.float32
            )
        return total

    totals = [located(shuffles_ref, p, 0) for p in range(perms)]
    mom_copy.wait_recv()
    for q in range(4):
        lines = slice(q * 128, (q + 1) * 128)
        total = mom_ref[lines, :] + mom_other[lines, :]
        square, cross, inter = total[:, 0:1], total[:, 1:2], total[:, 2:3]
        regression = cross / square
        divisor = inter - cross * regression + 0.1 * inter
        reg_ref[lines, :] = jnp.broadcast_to(regression, (128, 128))
        div_ref[:, lines] = jnp.transpose(jnp.broadcast_to(divisor, (128, 128)))[0:8, :]

    def own_residuals(k, _):
        residuals(g_ref, env_ref, reg_ref, h_ref, k, 0)
        return 0

    lax.fori_loop(0, half // 256, own_residuals, 0)
    second_hops(0)
    shuffle_copy.wait_recv()
    for p in range(perms):
        total = totals[p] + located(shuffles_other, p, half)
        spot = (total[:rows] * 128.0 + total[rows:]).astype(jnp.int32)
        inv_ref[p * rows : (p + 1) * rows, :] = jnp.minimum(jnp.maximum(spot, 0), 2 * half - 1) * 4

    index_rows = 1024
    blocks = 4 * half // index_rows

    def index_load(ref, slot, k):
        return pltpu.make_async_copy(
            inv_ref.at[pl.ds(pl.multiple_of(k * 8, 8), 8), :], ref, index_sem.at[slot]
        )

    index_load(index0, 0, 0).start()
    index_load(index1, 1, 1).start()

    def other_residuals(k, _):
        residuals(other_ref, env_other, reg_ref, h_ref, k, half)
        return 0

    env_copy.wait_recv()
    for copy in g_copies:
        copy.wait_recv()
    lax.fori_loop(0, half // 256, other_residuals, 0)
    second_hops(1)

    def right_side(ref, first, b, count):
        return jnp.concatenate(
            [ref[pl.ds(first + 2 * b + i, count, stride=4), :] for i in range(2)], axis=1
        ).astype(jnp.bfloat16)

    def gather(stage, index, offset):
        for t in range(STEP):
            stage[4 * t : 4 * t + 4, :] = h_ref[pl.ds(index[(offset + t) // 128, (offset + t) % 128], 4), :]

    def settle(stage, n):
        for q in range(4):
            gp_ref[pl.ds(pl.multiple_of((n + 1) * STEP, STEP), STEP), 128 * q : 128 * q + 128] = (
                stage[pl.ds(q, STEP, stride=4), :].astype(jnp.bfloat16)
            )

    def product(acc, rows, label, k, base, plain):
        start = pl.multiple_of(k * FAR_STEP, FAR_STEP)
        for b in range(2):
            lhs = band_ref[rows[b] : rows[b] + 256, pl.ds(start, FAR_STEP)]
            if plain:
                rhs = right_side(h_ref, start * 4, b, FAR_STEP)
            else:
                rhs = gp_ref[pl.ds(pl.multiple_of(base + start, STEP), FAR_STEP), 256 * b : 256 * b + 256]
            acc[2 * label + b] += jnp.dot(lhs, rhs, preferred_element_type=jnp.float32)

    near_rows, far_rows = (0, 64), (320, 320)

    def permuted(i, _, plain=False):
        for s, (index, slot) in enumerate(((index0, 0), (index1, 1))):
            index_load(index, slot, 2 * i + s).wait()
            n = 4 * i + 2 * s
            gather(stage0, index, 0)
            settle(stage1, n - 1)
            label = lax.div(i, 2)
            product(near_acc, near_rows, label, lax.rem(2 * i + s, 4), STEP + (label - 1) * half, plain)
            gather(stage1, index, STEP)
            settle(stage0, n)
            index_load(index, slot, lax.rem(2 * i + s + 2, blocks)).start()
        return 0

    lax.fori_loop(0, 2, functools.partial(permuted, plain=True), 0)
    lax.fori_loop(2, SPLIT, permuted, 0)
    third_hops()
    lax.fori_loop(SPLIT, blocks // 2, permuted, 0)
    settle(stage1, 4 * half // STEP - 1)
    index_load(index0, 0, 0).wait()
    index_load(index1, 1, 1).wait()

    def last_near(k, _):
        product(near_acc, near_rows, 4, k, STEP + 3 * half, False)
        return 0

    lax.fori_loop(0, half // FAR_STEP, last_near, 0)

    partials = []
    for label in range(5):
        copy = remote(
            near_acc.at[2 * label + 1 - core], near_in.at[label], p_send.at[label], p_recv.at[label], sib
        )
        copy.start()
        partials.append(copy)
    last_arrivals()

    for label in range(5):
        def distant(k, _, label=label):
            product(far_acc, far_rows, label, k, STEP + (label - 1) * half, label == 0)
            return 0

        lax.fori_loop(0, half // FAR_STEP, distant, 0)
        copy = remote(
            far_acc.at[2 * label + 1 - core], far_in.at[label], p_send.at[5 + label], p_recv.at[5 + label], sib
        )
        copy.start()
        partials.append(copy)

    divisor = div_ref[0:1, pl.ds(pl.multiple_of(core * 256, 256), 256)]
    lanes = lax.broadcasted_iota(jnp.int32, (256, 128), 1)
    for part, (acc, arrived) in enumerate(((near_acc, near_in), (far_acc, far_in))):
        peaks = jnp.zeros((256, 128), jnp.float32)
        for label in range(5):
            partials[5 * part + label].wait_recv()
            numerator = acc[2 * label + core] + arrived[label]
            scores = numerator * numerator / divisor
            peaks = jnp.where(lanes == label, jnp.max(scores, axis=1, keepdims=True), peaks)
        peak_ref[:, 256 * part : 256 * part + 128] = jnp.transpose(peaks[0:128])[0:8, :]
        peak_ref[:, 256 * part + 128 : 256 * part + 256] = jnp.transpose(peaks[128:256])[0:8, :]
    msg_ref[...] = jnp.zeros_like(msg_ref)
    shifts = [sum(jnp.where(place == x, SLOTS[x][slot], 0) for x in range(4)) for slot in range(9)]
    block = me * (snps // SNP_BLOCK) + core
    total_blocks = indices * (snps // SNP_BLOCK)
    for s in range(8):
        shift = jnp.where(core == 0, shifts[CORE_SLOTS[0][s]], shifts[CORE_SLOTS[1][s]])
        owner = jnp.clip(me + shift, 0, indices - 1)
        odd = lax.rem(owner, 2) == 1
        begin = start_ref[pl.ds(lax.div(owner, 2), 1), :]
        finish = end_ref[pl.ds(lax.div(owner, 2), 1), :]
        begin = jnp.where(odd, begin[:, 64:128], begin[:, 0:64])
        finish = jnp.where(odd, finish[:, 64:128], finish[:, 0:64])
        middle = (begin + finish - 1) >> 1
        lower = jnp.zeros_like(middle)
        upper = jnp.full_like(middle, total_blocks)
        for k in range(bounds_ref.shape[0]):
            bound = bounds_ref[k]
            before = bound <= middle
            lower = jnp.maximum(lower, jnp.where(before, bound, 0))
            upper = jnp.minimum(upper, jnp.where(before, total_blocks, bound))
        inner = (jnp.maximum(begin, lower) <= block) & (block < jnp.minimum(finish, upper))
        msg_ref[s, :, 0:64] = jnp.where(inner, peak_ref[:, 64 * s : 64 * s + 64], 0.0)

    sends = []
    for c in range(2):
        for s in range(8):
            for k in range(2):
                local = CORE_SLOTS[c][s] == 2
                if local and k == c:
                    continue
                shift = shifts[CORE_SLOTS[c][s]]
                copy = remote(
                    msg_ref.at[s], msg_in.at[2 * (shift + 4) + c], m_send.at[2 * s + k],
                    m_recv.at[2 * (shift + 4) + c], (me + shift, k),
                )
                condition = (core == c) & inside(shift)
                when(condition, copy.start)
                sends.append((condition, copy))

    best = jnp.where(core == 0, msg_ref[2], msg_ref[1])
    for c in range(2):
        for o in range(-4 + c, 4 + c):
            index = 2 * (o + 4) + c
            condition = (core == 1 - c) if o == 0 else inside(-o)
            copy = remote(msg_ref.at[0], msg_in.at[index], m_send.at[0], m_recv.at[index], sib)
            when(condition, copy.wait_recv)
            best = jnp.maximum(best, jnp.where(condition, msg_in[index], 0.0))
    pow_copy.wait_recv()
    power = pow_ref[...] + pow_other[...]
    result = jnp.sqrt(best / (power / (2.0 * half) + 1e-05))
    out_ref[...] = result[0:5, 0:64]

    for copy in g_copies + [shuffle_copy, env_copy, mom_copy, pow_copy] + partials:
        copy.wait_send()
    finish_hops()
    for condition, copy in sends:
        when(condition, copy.wait_send)


def shards(genotypes, phenotypes, environment, shuffles, window_start, window_end, chrom_bounds):
    snps, half = genotypes.shape
    genes = phenotypes.shape[0]
    labels = shuffles.shape[0] + 1
    vmem = pl.BlockSpec(memory_space=pltpu.VMEM)

    f32, bf16, i32 = jnp.float32, jnp.bfloat16, jnp.int32
    dma = pltpu.SemaphoreType.DMA
    shape = jax.ShapeDtypeStruct
    anywhere = pl.BlockSpec(memory_space=pl.ANY)
    smem = pl.BlockSpec(memory_space=pltpu.SMEM)
    weights = environment.reshape(-1, 128)
    lines = half // 128
    return pl.pallas_call(
        scan_kernel,
        name="scan",
        out_shape=shape((labels, genes), f32),
        in_specs=[smem] + [vmem] * 4 + [anywhere] * 2,
        out_specs=vmem,
        scratch_shapes=[
            pltpu.SMEM((8, 128), i32),
            pltpu.SMEM((8, 128), i32),
            pltpu.VMEM((2 * half * 4, 128), f32),
            pltpu.VMEM((4 * half + STEP, snps), bf16),
            pltpu.VMEM((9 * genes, half), bf16),
            pltpu.VMEM((snps, half), bf16),
            pltpu.VMEM((snps, half), bf16),
            pltpu.VMEM((labels - 1, half), i32),
            pltpu.VMEM((lines, 128), f32),
            pltpu.VMEM(((labels - 1) * lines, 128), i32),
            pltpu.VMEM((snps, 128), f32),
            pltpu.VMEM((snps, 128), f32),
            pltpu.VMEM((snps, 128), f32),
            pltpu.VMEM((8, snps), f32),
            pltpu.VMEM((8, 128), f32),
            pltpu.VMEM((8, 128), f32),
            pltpu.VMEM((4 * STEP, 128), f32),
            pltpu.VMEM((4 * STEP, 128), f32),
            pltpu.VMEM((2 * labels, 256, 256), f32),
            pltpu.VMEM((2 * labels, 256, 256), f32),
            pltpu.VMEM((labels, 256, 256), f32),
            pltpu.VMEM((labels, 256, 256), f32),
            pltpu.VMEM((8, 8 * genes), f32),
            pltpu.VMEM((8, 8, 128), f32),
            pltpu.VMEM((18, 8, 128), f32),
            dma((20,)), dma((18,)), dma((4,)), dma((4,)), dma((4,)), dma((4,)),
            dma((10,)), dma((10,)), dma((16,)), dma((18,)), dma((5,)), dma((2,)),
        ],
        compiler_params=pltpu.CompilerParams(
            collective_id=0, has_side_effects=True, vmem_limit_bytes=64 * 1024 * 1024 - 65536
        ),
    )(
        chrom_bounds, shuffles, weights, window_start.reshape(-1, 128), window_end.reshape(-1, 128),
        phenotypes, genotypes,
    )


def solution(mesh):
    placed = (
        P("genome", "sample"),
        P("genome", "sample"),
        P("sample"),
        P(None, "sample"),
        P(),
        P(),
        P(),
    )
    return jax.shard_map(
        shards, mesh=mesh, in_specs=placed, out_specs=P(None, "genome"), check_vma=False
    )
```

time: 73.9 us -> 60.6 us (0.82)
  Pallas kernels: 70 us -> 59.2 us
  waiting for transfers between devices: 1.11 us -> 0 us
    pallas_call x2 -> x1, Pallas kernels: 70 us -> 59.2 us  [shards(): pl.pallas_call(scan_kernel, name='scan', out_shape=shape((labels, genes),...]
    ppermute x1 -> x0, waiting for transfers between devices: 1.11 us -> none  [shards(): shuffles_other = lax.ppermute(shuffles, 'sample', [(0, 1), (1, 0)])]
    unnamed x3 -> x1, local copies, waits for them, and re-layouts: 1.89 us -> 1.28 us
  transfers between devices with their start and end apart: 1 -> 0, of which waited for: 1 -> 0; matrix products, arithmetic and copies ran while one was open for 0% -> 0% of each run, Pallas kernels for 0% -> 0%
where the time goes in v4:
time: 60.6 us; the launch traced here: 60.4 us
  Pallas kernels  59.2 us (98%)
  local copies, waits for them, and re-layouts  1.28 us (2%)
    pallas_call x1, Pallas kernels, shards(): pl.pallas_call(scan_kernel, name='scan', out_shape=shape((labels, genes),...  59.2 us
    unnamed x1, local copies, waits for them, and re-layouts  1.28 us

profile of v4, /device:TPU:97, one launch (start us, length us, event | category | flops | bytes accessed | tf_op | source)
XLA Modules:
  0.0 60.4 jit_solution(12325608719430848173)
XLA Ops:
  0.0 59.2 %scan.1 = f32[5,64]{1,0:T(8,128)} custom-call(s32[21]{0:T(128)} %bounds_ref.1, s32[4,4096]{1,0:T(4,128)} %shuffles_ref.1, f32[32,128]{1,0:T(8,128)} %bitcast.3, s32[32,128]{1,0:T(8,128)} %bitcast.4, s32[32,128]{1,0:T(8,128)} %bitcast.5, bf16[64,4096]{1,0:T(8,128)(2,1)} %y_hbm.1, bf16[512,4096]{1,0:T(8,128)(2,1)} %g_hbm.1), custom_call_target="tpu_custom_call" | custom-call | tf_op jit(solution)/shard_map/scan/pallas_call | solution.py:489
  59.2 1.3 %copy.9 = f32[5,64]{1,0:T(8,128)} copy(f32[5,64]{1,0:T(8,128)} %scan.1) | data formatting | bytes 2560

commit v5 on v4

--- a/solution.py
+++ b/solution.py
@@ -42,7 +42,7 @@
             rows = slice(q * 128, (q + 1) * 128)
             value = source[rows, pl.ds(start, 128)].astype(jnp.float32)
             value = jnp.transpose(value * (weight - reg_ref[rows, :]))
-            h_ref[pl.ds((first + start) * 4 + q, 128, stride=4), :] = value
+            h_ref[pl.ds((first + start) * 4 + 4 + q, 128, stride=4), :] = value
 
 
 def scan_kernel(
@@ -305,7 +305,7 @@
     for p in range(perms):
         total = totals[p] + located(shuffles_other, p, half)
         spot = (total[:rows] * 128.0 + total[rows:]).astype(jnp.int32)
-        inv_ref[p * rows : (p + 1) * rows, :] = jnp.minimum(jnp.maximum(spot, 0), 2 * half - 1) * 4
+        inv_ref[p * rows : (p + 1) * rows, :] = jnp.minimum(jnp.maximum(spot, 0), 2 * half - 1) * 4 + 4
 
     index_rows = 1024
     blocks = 4 * half // index_rows
@@ -333,22 +333,28 @@
             [ref[pl.ds(first + 2 * b + i, count, stride=4), :] for i in range(2)], axis=1
         ).astype(jnp.bfloat16)
 
-    def gather(stage, index, offset):
-        for t in range(STEP):
-            stage[4 * t : 4 * t + 4, :] = h_ref[pl.ds(index[(offset + t) // 128, (offset + t) % 128], 4), :]
-
-    def settle(stage, n):
+    run = 64
+    is_upper = lax.broadcasted_iota(jnp.int32, (8, 128), 0) < 4
+
+    def gather(stage, index, offset, first):
+        for t in range(first, first + run, 2):
+            row = offset + t
+            upper = h_ref[pl.ds(index[row // 128, row % 128], 8), :]
+            lower = h_ref[pl.ds(index[row // 128, row % 128 + 1] - 4, 8), :]
+            stage[4 * t : 4 * t + 8, :] = jnp.where(is_upper, upper, lower)
+
+    def settle(stage, n, first):
         for q in range(4):
-            gp_ref[pl.ds(pl.multiple_of((n + 1) * STEP, STEP), STEP), 128 * q : 128 * q + 128] = (
-                stage[pl.ds(q, STEP, stride=4), :].astype(jnp.bfloat16)
+            gp_ref[pl.ds(pl.multiple_of((n + 1) * STEP + first, run), run), 128 * q : 128 * q + 128] = (
+                stage[pl.ds(4 * first + q, run, stride=4), :].astype(jnp.bfloat16)
             )
 
-    def product(acc, rows, label, k, base, plain):
+    def product(acc, rows, label, k, base, plain, blocks=(0, 1)):
         start = pl.multiple_of(k * FAR_STEP, FAR_STEP)
-        for b in range(2):
+        for b in blocks:
             lhs = band_ref[rows[b] : rows[b] + 256, pl.ds(start, FAR_STEP)]
             if plain:
-                rhs = right_side(h_ref, start * 4, b, FAR_STEP)
+                rhs = right_side(h_ref, start * 4 + 4, b, FAR_STEP)
             else:
                 rhs = gp_ref[pl.ds(pl.multiple_of(base + start, STEP), FAR_STEP), 256 * b : 256 * b + 256]
             acc[2 * label + b] += jnp.dot(lhs, rhs, preferred_element_type=jnp.float32)
@@ -359,12 +365,14 @@
         for s, (index, slot) in enumerate(((index0, 0), (index1, 1))):
             index_load(index, slot, 2 * i + s).wait()
             n = 4 * i + 2 * s
-            gather(stage0, index, 0)
-            settle(stage1, n - 1)
             label = lax.div(i, 2)
-            product(near_acc, near_rows, label, lax.rem(2 * i + s, 4), STEP + (label - 1) * half, plain)
-            gather(stage1, index, STEP)
-            settle(stage0, n)
+            k = lax.rem(2 * i + s, 4)
+            base = STEP + (label - 1) * half
+            for b, (stage, before) in enumerate(((stage0, stage1), (stage1, stage0))):
+                product(near_acc, near_rows, label, k, base, plain, (b,))
+                for first in range(0, STEP, run):
+                    settle(before, n - 1 + b, first)
+                    gather(stage, index, b * STEP, first)
             index_load(index, slot, lax.rem(2 * i + s + 2, blocks)).start()
         return 0
 
@@ -372,7 +380,8 @@
     lax.fori_loop(2, SPLIT, permuted, 0)
     third_hops()
     lax.fori_loop(SPLIT, blocks // 2, permuted, 0)
-    settle(stage1, 4 * half // STEP - 1)
+    for first in range(0, STEP, run):
+        settle(stage1, 4 * half // STEP - 1, first)
     index_load(index0, 0, 0).wait()
     index_load(index1, 1, 1).wait()
 
@@ -495,7 +504,7 @@
         scratch_shapes=[
             pltpu.SMEM((8, 128), i32),
             pltpu.SMEM((8, 128), i32),
-            pltpu.VMEM((2 * half * 4, 128), f32),
+            pltpu.VMEM((2 * half * 4 + 8, 128), f32),
             pltpu.VMEM((4 * half + STEP, snps), bf16),
             pltpu.VMEM((9 * genes, half), bf16),
             pltpu.VMEM((snps, half), bf16),

time: 60.6 us -> 60.4 us (level)
  no operation moved by 1% of the time
where the time goes in v5:
time: 60.4 us; the launch traced here: 60.2 us
  Pallas kernels  59 us (98%)
  local copies, waits for them, and re-layouts  1.28 us (2%)
    pallas_call x1, Pallas kernels, shards(): pl.pallas_call(scan_kernel, name='scan', out_shape=shape((labels, genes),...  59 us
    unnamed x1, local copies, waits for them, and re-layouts  1.28 us

profile of v5, /device:TPU:97, one launch (start us, length us, event | category | flops | bytes accessed | tf_op | source)
XLA Modules:
  0.0 60.2 jit_solution(5091061706671612510)
XLA Ops:
  0.0 59.0 %scan.1 = f32[5,64]{1,0:T(8,128)} custom-call(s32[21]{0:T(128)} %bounds_ref.1, s32[4,4096]{1,0:T(4,128)} %shuffles_ref.1, f32[32,128]{1,0:T(8,128)} %bitcast.3, s32[32,128]{1,0:T(8,128)} %bitcast.4, s32[32,128]{1,0:T(8,128)} %bitcast.5, bf16[64,4096]{1,0:T(8,128)(2,1)} %y_hbm.1, bf16[512,4096]{1,0:T(8,128)(2,1)} %g_hbm.1), custom_call_target="tpu_custom_call" | custom-call | tf_op jit(solution)/shard_map/scan/pallas_call | solution.py:498
  59.0 1.3 %copy.9 = f32[5,64]{1,0:T(8,128)} copy(f32[5,64]{1,0:T(8,128)} %scan.1) | data formatting | bytes 2560
